TPU v7x, 128 devices: a whole 4x4x4 slice. The times are simulated.
128 devices in a mesh: dp: 8 (over y, core), expert: 16 (over z, x).
Axes of the slice: x: 4, y: 4, z: 4, core: 2. Of those that a mesh axis runs over, the one named last changes fastest.
Arguments:
- tokens: bfloat16 [2048, 4096], P('expert', 'dp'), may hold values from -6 to 6
- grad_out: bfloat16 [2048, 4096], P('expert', 'dp'), may hold values from -6 to 6
- expert_ids: int32 [2048, 8], P('expert'), may hold values from 0 to 63, all different within a row; in each aligned block of 128 rows (0 to 127, 128 to 255, ...) at most 24 rows name the same one
- gate_probs: float32 [2048, 8], P('expert'), may hold values from 0.05 to 0.3
- seq_ids: int32 [2048], P('expert'), may hold values from 0 to 7, never falling along the last dimension, each value on 1 to 1024 neighbouring positions
- log_ratio: float32 [2048], P('expert'), may hold values from -8 to 8
- advantages: float32 [8], replicated, may hold values from -4 to 4
- w_gate: bfloat16 [64, 1536, 4096], P('expert', 'dp'), may hold values from -0.09375 to 0.09375
- w_up: bfloat16 [64, 1536, 4096], P('expert', 'dp'), may hold values from -0.09375 to 0.09375
- w_down: bfloat16 [64, 1536, 4096], P('expert', 'dp'), may hold values from -0.09375 to 0.09375
Outputs:
- grad_tokens: bfloat16 [2048, 4096], P('expert', 'dp')
- grad_gates: float32 [2048, 8], P('expert')
- grad_down: bfloat16 [64, 1536, 4096], P('expert', 'dp')
Inputs may be any that keep to these rules, and one draw needn't show every extreme that they name: `expert_ids`: each row names 8 different experts; among the rows of one index of expert no expert is named more than 24 times, a bound that some block reaches. `seq_ids`: never falling; every sequence has 1 to 1024 tokens and one has exactly 1024.
All inputs are finite; a program needn't handle non-finite values.
Results may differ from a plain program's by a relative error of at most 0.023.
Values may be sent and summed in bfloat16 or wider, within the bound.
A program may use at most 192 MiB of HBM per device.

v0:
```python
import jax
import jax.numpy as jnp
from jax import lax
from jax.sharding import PartitionSpec as P

SEQS = 8


clip_low = 0.9
clip_high = 1.1


def on_device(
    tokens, grad_out, expert_ids, gate_probs, seq_ids, log_ratio, advantages, w_gate, w_up, w_down
):
    count_tok = expert_ids.shape[0]
    top_k = expert_ids.shape[1]
    groups = lax.axis_size("expert")
    local = w_gate.shape[0]
    experts = local * groups
    capacity = count_tok * top_k * 3 // (2 * experts)
    onehot_seq = (seq_ids[:, None] == jnp.arange(SEQS, dtype=jnp.int32)[None, :]).astype(
        jnp.float32
    )
    local_sums = jnp.dot(log_ratio, onehot_seq, precision=lax.Precision.HIGHEST)
    local_counts = jnp.sum(onehot_seq, axis=0)
    sums, counts = lax.psum((local_sums, local_counts), "expert")
    clipped = jnp.clip(jnp.exp(sums / counts), clip_low, clip_high)
    seq_weight = advantages * clipped
    token_weight = jnp.dot(onehot_seq, seq_weight, precision=lax.Precision.HIGHEST)
    coef = token_weight[:, None] * gate_probs
    flat_ids = expert_ids.reshape(-1)
    route_hot = (flat_ids[:, None] == jnp.arange(experts, dtype=jnp.int32)[None, :]).astype(
        jnp.int32
    )
    earlier = jnp.cumsum(route_hot, axis=0) - route_hot
    slot_of = jnp.sum(earlier * route_hot, axis=1)
    dest = flat_ids * capacity + slot_of
    token_of = jnp.arange(count_tok * top_k, dtype=jnp.int32) // top_k

    def place(rows):
        buffer = jnp.zeros((experts * capacity, rows.shape[1]), rows.dtype)
        return buffer.at[dest].set(rows[token_of]).reshape(experts, capacity, rows.shape[1])

    coef_buf = (
        jnp.zeros((experts * capacity,), jnp.float32)
        .at[dest]
        .set(coef.reshape(-1))
        .reshape(experts, capacity)
    )
    full_x, full_dy = (
        lax.all_gather(tokens, "dp", axis=1, tiled=True),
        lax.all_gather(grad_out, "dp", axis=1, tiled=True),
    )
    xs, dys, coefs = (
        lax.all_to_all(place(full_x), "expert", split_axis=0, concat_axis=0, tiled=True),
        lax.all_to_all(place(full_dy), "expert", split_axis=0, concat_axis=0, tiled=True),
        lax.all_to_all(
            coef_buf.astype(jnp.bfloat16), "expert", split_axis=0, concat_axis=0, tiled=True
        ).astype(coef_buf.dtype),
    )
    width = xs.shape[2]
    xs = xs.reshape(groups, local, capacity, width)
    dys = dys.reshape(groups, local, capacity, width)
    coefs = coefs.reshape(groups, local, capacity)
    g = jnp.einsum("snrd,nfd->snrf", xs, w_gate, preferred_element_type=jnp.float32)
    u = jnp.einsum("snrd,nfd->snrf", xs, w_up, preferred_element_type=jnp.float32)
    sg = jax.nn.sigmoid(g)
    hidden = (g * sg * u).astype(jnp.bfloat16)
    z = jnp.einsum("snrd,nfd->snrf", dys, w_down, preferred_element_type=jnp.float32)
    dh = coefs[..., None] * z
    dg = (dh * u * sg * (1.0 + g * (1.0 - sg))).astype(jnp.bfloat16)
    du = (dh * g * sg).astype(jnp.bfloat16)
    scaled = (coefs[..., None] * dys.astype(jnp.float32)).astype(jnp.bfloat16)
    grad_down = jnp.einsum(
        "snrf,snrd->nfd", hidden, scaled, preferred_element_type=jnp.float32
    ).astype(jnp.bfloat16)
    gate_part = jnp.sum(hidden.astype(jnp.float32) * z, axis=3)
    part = jnp.einsum("snrf,nfd->snrd", dg, w_gate, preferred_element_type=jnp.float32)
    part = part + jnp.einsum("snrf,nfd->snrd", du, w_up, preferred_element_type=jnp.float32)
    summed = lax.psum_scatter(
        part.astype(jnp.bfloat16), "dp", scatter_dimension=3, tiled=True
    ).astype(jnp.float32)
    gate_full = lax.psum(gate_part, "dp")
    cols = summed.shape[3]
    back_dx, back_gate = (
        lax.all_to_all(
            summed.reshape(experts, capacity, cols).astype(jnp.bfloat16),
            "expert",
            split_axis=0,
            concat_axis=0,
            tiled=True,
        ).astype(jnp.float32),
        lax.all_to_all(
            gate_full.reshape(experts, capacity).astype(jnp.bfloat16),
            "expert",
            split_axis=0,
            concat_axis=0,
            tiled=True,
        ).astype(jnp.float32),
    )
    route_dx = back_dx.reshape(experts * capacity, cols)[dest]
    token_dx = jnp.sum(route_dx.reshape(count_tok, top_k, cols), axis=1)
    route_gate = back_gate.reshape(-1)[dest].reshape(count_tok, top_k)
    grad_gates = token_weight[:, None] * route_gate
    return (token_dx.astype(jnp.bfloat16), grad_gates, grad_down)


def solution(mesh):
    return jax.shard_map(
        on_device,
        mesh=mesh,
        in_specs=(
            P("expert", "dp"),
            P("expert", "dp"),
            P("expert", None),
            P("expert", None),
            P("expert"),
            P("expert"),
            P(),
            P("expert", "dp", None),
            P("expert", "dp", None),
            P("expert", "dp", None),
        ),
        out_specs=(P("expert", "dp"), P("expert", None), P("expert", "dp", None)),
        check_vma=False,
    )
```

profile of v0, /device:TPU:0, one launch (start us, length us, event | category | flops | bytes accessed | tf_op | source)
XLA Modules:
  0.0 730.0 jit_solution(821476025868501675)
XLA Ops:
  7.2 0.7 all-gather.5.cloned.1.call-update
  7.9 0.8 copy.68
  8.7 0.1 eq.42
  8.8 0.1 eq.38
  8.9 0.7 broadcast_multiply_fusion.2
  9.6 0.1 copy.67
  9.7 0.1 mul.81
  9.8 18.0 %reduce-window.6 = s32[64,8,128]{2,1,0:T(8,128)S(1)} reduce-window(s32[64,8,128]{2,1,0:T(8,128)S(1)} %fusion.42, s32[]{:T(128)} %constant.30.clone.1), window={size=1x1x128 pad=0_0x0_0x127_0}, to_apply=%region_0.0 | reduce-window | flops 8323072 | bytes 524292 | tf_op jit(solution)/shard_map/reduce-window
  27.8 0.1 slice.16
  28.0 0.1 copy.70
  28.2 0.1 broadcast_add_fusion
  28.5 7.2 all-gather.5.cloned.1.call-done
  35.7 16.4 %gather_fusion.1 = bf16[1024,4096]{1,0:T(8,128)(2,1)} fusion(bf16[128,4096]{1,0:T(8,128)(2,1)} %all-gather.5.cloned.1.call-done, s32[1024]{0:T(1024)S(1)} %broadcast_clamp_fusion.1), kind=kCustom, calls=%fused_computation.1 | custom fusion | bytes 16781312 | tf_op jit(solution)/shard_map/gather | solution.py:43
  52.1 29.6 %scatter_custom_fusion.2 = bf16[1536,4096]{1,0:T(8,128)(2,1)} fusion(s32[1024]{0:T(1024)S(1)} %bitcast.133, bf16[1024,4096]{1,0:T(8,128)(2,1)} %gather_fusion.1, bf16[]{:T(256)} %constant.34.clone.1), kind=kCustom, calls=%fused_computation.25 | custom fusion | bytes 12583424 | tf_op jit(solution)/shard_map/scatter | solution.py:43
  81.7 7.0 all-to-all-start.2
  88.7 0.7 all-gather.3.cloned.1.call-update
  89.4 25.3 %all-gather.3.cloned.1.call-done = bf16[128,4096]{1,0:T(8,128)(2,1)} async-done(((bf16[128,512]{1,0:T(8,128)(2,1)}), bf16[128,4096]{1,0:T(8,128)(2,1)}) %all-gather.3.cloned.1.call-update) | async-done | bytes 1048592 | tf_op jit(solution)/shard_map/all_gather | solution.py:53
  114.8 16.5 %gather_fusion = bf16[1024,4096]{1,0:T(8,128)(2,1)} fusion(bf16[128,4096]{1,0:T(8,128)(2,1)} %all-gather.3.cloned.1.call-done, s32[1024]{0:T(1024)S(1)} %broadcast_clamp_fusion.1), kind=kCustom, calls=%fused_computation | custom fusion | bytes 16781312 | tf_op jit(solution)/shard_map/gather | solution.py:43
  131.2 20.1 %scatter_custom_fusion.1 = bf16[1536,4096]{1,0:T(8,128)(2,1)} fusion(s32[1024]{0:T(1024)S(1)} %bitcast.134, bf16[1024,4096]{1,0:T(8,128)(2,1)} %gather_fusion, bf16[]{:T(256)} %constant.34.clone.1), kind=kCustom, calls=%fused_computation.27 | custom fusion | bytes 12583424 | tf_op jit(solution)/shard_map/scatter | solution.py:43
  151.4 126.2 %all-to-all-done.2 = bf16[64,24,4096]{2,1,0:T(8,128)(2,1)} async-done(((bf16[64,24,4096]{2,1,0:T(8,128)(2,1)}), bf16[64,24,4096]{2,1,0:T(8,128)(2,1)}, u32[]{:S(2)}, u32[]{:S(2)}) %all-to-all-start.2) | async-done | bytes 12582944 | tf_op jit(solution)/shard_map/all_to_all | solution.py:56
  277.5 5.1 all-to-all-start.1
  282.7 0.1 convolution_bitcast_fusion.1
  282.8 0.1 convert_reduce_fusion
  282.9 212.0 %all-reduce = (f32[8]{0:T(128)S(1)}, f32[8]{0:T(128)S(1)}) all-reduce(f32[8]{0:T(128)S(1)} %convolution_bitcast_fusion.1, f32[8]{0:T(128)S(1)} %convert_reduce_fusion), channel_id=1, replica_groups=mesh['dp'=8,'expert'=16] {'expert'}, use_global_device_ids=true, to_apply=%region_3.4 | all-reduce | flops 16 | bytes 128 | tf_op jit(solution)/shard_map/psum | solution.py:27
  494.9 8.7 %fusion.5 = f32[4,16,24,192]{3,2,1,0:T(8,128)S(1)} fusion(bf16[16,4,24,4096]{3,2,1,0:T(8,128)(2,1)} %bitcast.15, bf16[4,192,4096]{2,1,0:T(8,128)(2,1)} %param.17), kind=kOutput, calls=%fused_computation.15 | convolution fusion | flops 2415919104 | bytes 20054016 | tf_op jit(solution)/shard_map/snrd,nfd->snrf/dot_general | solution.py:66
  503.7 11.0 %fusion.7 = f32[4,16,24,192]{3,2,1,0:T(8,128)} fusion(bf16[16,4,24,4096]{3,2,1,0:T(8,128)(2,1)} %bitcast.15, bf16[4,192,4096]{2,1,0:T(8,128)(2,1)} %param.18), kind=kOutput, calls=%fused_computation.17 | convolution fusion | flops 2415919104 | bytes 20054016 | tf_op jit(solution)/shard_map/snrd,nfd->snrf/dot_general | solution.py:67
  514.6 10.2 %fusion.32 = (f32[16,4,24]{2,0,1:T(8,128)S(1)}, bf16[16,4,24,192]{3,2,0,1:T(8,128)(2,1)}, f32[4,16,24,192]{3,2,1,0:T(8,128)S(1)}) fusion(f32[4,16,24,192]{3,2,1,0:T(8,128)} %fusion.7, f32[4,16,24,192]{3,2,1,0:T(8,128)S(1)} %fusion.5, bf16[4,192,4096]{2,1,0:T(8,128)(2,1)} %param.19, bf16[16,4,24,4096]{3,2,1,0:T(8,128)(2,1)} %bitcast.10), kind=kOutput, calls=%fused_computation.49 | convolution fusion | flops 2418571776 | bytes 23009280 | tf_op jit(solution)/shard_map/snrd,nfd->snrf/dot_general | solution.py:70
  524.8 23.6 %psum.23 = bf16[16,4,24]{2,0,1:T(8,128)(2,1)S(1)} all-reduce(f32[16,4,24]{2,0,1:T(8,128)S(1)} %get-tuple-element.20), channel_id=1, replica_groups=mesh['dp'=8,'expert'=16] {'dp'}, use_global_device_ids=true, to_apply=%region_12.13 | all-reduce | flops 1536 | bytes 9216 | tf_op jit(solution)/shard_map/psum | solution.py:84
  548.4 0.6 copy.78
  549.0 3.7 all-to-all-start.4
  552.8 0.1 convolution_bitcast_fusion
  552.9 0.1 copy.72
  553.0 7.2 all-to-all-done.4
  560.3 6.2 gather_fusion.3
  566.8 4.3 scatter_custom_fusion
  571.1 0.1 convert_element_type.73
  571.2 10.6 %all_to_all.27 = bf16[16,4,24]{2,1,0:T(4,128)(2,1)S(1)} all-to-all(bf16[16,4,24]{2,1,0:T(4,128)(2,1)S(1)} %convert_element_type.73), channel_id=1, replica_groups=mesh['dp'=8,'expert'=16] {'expert'}, dimensions={0} | all-to-all | bytes 6144 | tf_op jit(solution)/shard_map/all_to_all | solution.py:58
  581.8 15.3 %fusion.11 = f32[4,16,24,4096]{3,2,1,0:T(8,128)} fusion(bf16[4,192,4096]{2,1,0:T(8,128)(2,1)} %param.17, f32[4,16,24,192]{3,2,1,0:T(8,128)S(1)} %fusion.5, f32[4,16,24,192]{3,2,1,0:T(8,128)} %fusion.7, f32[4,16,24,192]{3,2,1,0:T(8,128)S(1)} %get-tuple-element.24, f32[16,4,24]{2,0,1:T(8,128)S(1)} %copy.73), kind=kOutput, calls=%fused_computation.19 | convolution fusion | flops 2419163136 | bytes 35002368 | tf_op jit(solution)/shard_map/snrf,nfd->snrd/dot_general | solution.py:79
  597.1 15.9 %fusion = bf16[16,4,24,4096]{3,2,0,1:T(8,128)(2,1)} fusion(f32[4,16,24,4096]{3,2,1,0:T(8,128)} %fusion.11, bf16[4,192,4096]{2,1,0:T(8,128)(2,1)} %param.18, f32[4,16,24,192]{3,2,1,0:T(8,128)S(1)} %fusion.5, f32[4,16,24,192]{3,2,1,0:T(8,128)S(1)} %get-tuple-element.24, f32[16,4,24]{2,0,1:T(8,128)S(1)} %copy.73), kind=kOutput, calls=%fused_computation.9 | convolution fusion | flops 2430566400 | bytes 46405632 | tf_op jit(solution)/shard_map/snrf,nfd->snrd/dot_general | solution.py:80
  613.0 0.7 copy.80
  613.7 66.9 %reduce-scatter.2.cloned.1.call-done = bf16[16,4,24,512]{3,2,0,1:T(8,128)(2,1)} async-done(((bf16[16,4,24,4096]{3,2,0,1:T(8,128)(2,1)}), bf16[16,4,24,512]{3,2,0,1:T(8,128)(2,1)}) %reduce-scatter.2.cloned.1.call-update) | async-done | bytes 1572880 | tf_op jit(solution)/shard_map/reduce_scatter | solution.py:81
  680.6 2.7 copy.77
  683.4 7.0 all-to-all-start.3
  690.4 8.4 %bitcast_convert_fusion = bf16[4,192,4096]{2,1,0:T(8,128)(2,1)} fusion(bf16[16,4,24,192]{3,2,0,1:T(8,128)(2,1)S(1)} %copy-done.5, f32[16,4,24]{2,1,0:T(4,128)S(1)} %convert_element_type.74, bf16[64,24,4096]{2,1,0:T(8,128)(2,1)} %all-to-all-done.1), kind=kOutput, calls=%fused_computation.10 | convolution fusion | flops 2437939200 | bytes 19470336 | tf_op jit(solution)/shard_map/snrf,snrd->nfd/dot_general | solution.py:75
  698.8 15.0 %all-to-all-done.3 = bf16[64,24,512]{2,1,0:T(8,128)(2,1)} async-done(((bf16[64,24,512]{2,1,0:T(8,128)(2,1)}), bf16[64,24,512]{2,1,0:T(8,128)(2,1)}, u32[]{:S(2)}, u32[]{:S(2)}) %all-to-all-start.3) | async-done | bytes 1572896 | tf_op jit(solution)/shard_map/all_to_all | solution.py:87
  713.8 1.9 bitcast_convert_fusion.1
  715.7 4.9 gather_fusion.2
  720.6 2.8 bitcast_reduce_fusion
  (33 shorter events, 0.8 us)
Async XLA Ops:
  7.2 275.5 %copy-start = (f32[128]{0:T(128)S(1)}, f32[128]{0:T(128)}, u32[]{:S(2)}) copy-start(f32[128]{0:T(128)} %param.15) | copy-start | bytes 1540
  7.2 28.5 %all-gather.5.cloned.1.call-start = ((), (), s32[]{:S(2)}) async-start(), calls=%async_computation.7 | async-start | bytes 1179648 | tf_op jit(solution)/shard_map/all_gather | solution.py:52
  81.7 195.8 %all-to-all-start.2 = ((bf16[64,24,4096]{2,1,0:T(8,128)(2,1)}), bf16[64,24,4096]{2,1,0:T(8,128)(2,1)}, u32[]{:S(2)}, u32[]{:S(2)}) async-start(bf16[64,24,4096]{2,1,0:T(8,128)(2,1)} %bitcast.128), calls=%async_computation.2 | async-start | bytes 25165824 | tf_op jit(solution)/shard_map/all_to_all | solution.py:56
  88.7 26.1 %all-gather.3.cloned.1.call-start = ((), (), s32[]{:S(2)}) async-start(), calls=%async_computation.6 | async-start | bytes 1179648 | tf_op jit(solution)/shard_map/all_gather | solution.py:53
  277.5 5.1 copy-start.3
  277.5 237.1 %all-to-all-start.1 = ((bf16[64,24,4096]{2,1,0:T(8,128)(2,1)}), bf16[64,24,4096]{2,1,0:T(8,128)(2,1)}, u32[]{:S(2)}, u32[]{:S(2)}) async-start(bf16[64,24,4096]{2,1,0:T(8,128)(2,1)} %bitcast.129), calls=%async_computation.1 | async-start | bytes 25165824 | tf_op jit(solution)/shard_map/all_to_all | solution.py:57
  514.6 38.1 %copy-start.4 = (f32[8]{0:T(128)S(1)}, f32[8]{0:T(128)}, u32[]{:S(2)}) copy-start(f32[8]{0:T(128)} %param.16) | copy-start | bytes 100
  514.6 38.3 %copy-start.2 = (f32[128,8]{0,1:T(8,128)S(1)}, f32[128,8]{0,1:T(8,128)}, u32[]{:S(2)}) copy-start(f32[128,8]{0,1:T(8,128)} %param.13) | copy-start | bytes 12292
  549.0 11.2 %all-to-all-start.4 = ((bf16[16,4,24]{2,1,0:T(4,128)(2,1)}), bf16[16,4,24]{2,1,0:T(4,128)(2,1)S(1)}, u32[]{:S(2)}, u32[]{:S(2)}) async-start(bf16[16,4,24]{2,1,0:T(4,128)(2,1)} %copy.78), calls=%async_computation.5 | async-start | bytes 32768 | tf_op jit(solution)/shard_map/all_to_all | solution.py:94
  552.7 127.9 %reduce-scatter.2.cloned.1.call-start = ((), (), s32[]{:S(2)}) async-start(), calls=%async_computation.8 | async-start | bytes 14155776 | tf_op jit(solution)/shard_map/reduce_scatter | solution.py:81
  613.0 77.4 %copy-start.5 = (bf16[16,4,24,192]{3,2,0,1:T(8,128)(2,1)S(1)}, bf16[16,4,24,192]{3,2,0,1:T(8,128)(2,1)}, u32[]{:S(2)}) copy-start(bf16[16,4,24,192]{3,2,0,1:T(8,128)(2,1)} %get-tuple-element.21) | copy-start | bytes 1769476
  683.4 30.4 %all-to-all-start.3 = ((bf16[64,24,512]{2,1,0:T(8,128)(2,1)}), bf16[64,24,512]{2,1,0:T(8,128)(2,1)}, u32[]{:S(2)}, u32[]{:S(2)}) async-start(bf16[64,24,512]{2,1,0:T(8,128)(2,1)} %bitcast.24), calls=%async_computation.4 | async-start | bytes 3145728 | tf_op jit(solution)/shard_map/all_to_all | solution.py:87
  713.8 9.5 %copy-start.1 = (f32[128]{0:T(128)S(1)}, f32[128]{0:T(128)}, u32[]{:S(2)}) copy-start(f32[128]{0:T(128)} %param.15) | copy-start | bytes 1540
Sparse Core Ops, SparseCore 0:
  9.7 25.9 all-gather.4
  91.2 23.4 all-gather.2
  613.1 67.4 reduce-scatter.1
where the time goes:
time: 736 us; the launch traced here: 730 us
  waiting for transfers between devices  249 us (34%)
  blocking collectives  246 us (33%)
  local copies, waits for them, and re-layouts  104 us (14%)
  matrix products  69.6 us (9%)
  other arithmetic  23.8 us (3%)
  starting transfers between devices  22.9 us (3%)
  between operations  14.2 us (2%)
    psum x1, blocking collectives, on_device(): sums, counts = lax.psum((local_sums, local_counts), 'expert')  212 us
    all_to_all x1, waiting for transfers between devices, on_device(): lax.all_to_all(place(full_x), 'expert', split_axis=0, concat_axis=0, tile...  126 us
    reduce_scatter x1, waiting for transfers between devices, on_device(): lax.psum_scatter(part.astype(jnp.bfloat16), 'dp', scatter_dimension=3, ti...  66.9 us
    scatter x2, local copies, waits for them, and re-layouts, place(): buffer.at[dest].set(rows[token_of])  49.8 us
    gather x2, local copies, waits for them, and re-layouts, place(): rows[token_of]  32.9 us
    all_gather x1, waiting for transfers between devices, on_device(): lax.all_gather(grad_out, 'dp', axis=1, tiled=True)  25.3 us
    psum x1, blocking collectives, on_device(): gate_full = lax.psum(gate_part, 'dp')  23.6 us
    another operation x3, other arithmetic  18.2 us
  transfers between devices with their start and end apart: 7, of which 6 were waited for; matrix products, arithmetic and copies ran while one was open for 12% of the time, Pallas kernels for 0%

commit v1 on v0

v1 whole, which is shorter than its diff:
```python
import jax
import jax.numpy as jnp
from jax import lax
from jax.experimental import pallas as pl
from jax.experimental.pallas import tpu as pltpu
from jax.sharding import PartitionSpec as P

SEQS = 8
TOP = 8
CAP = 24
clip_low = 0.9
clip_high = 1.1

MESH = pl.DeviceIdType.MESH
BF = jnp.bfloat16
F32 = jnp.float32
PARTS = ((0, 176, 96), (176, 176, 80), (352, 160, 80))
ORDER = ((0, 1, 2), (1, 2, 0), (2, 0, 1))
BASE = (0, 1, 5)
COUNT = (1, 4, 16)
NT = (((1,), (1,)), ((), ()))
TN = (((0,), (0,)), ((), ()))


def group(a, b):
    return b * 4 + a


def step_kernel(
    adv, tok, gout, meta, wg, wu, wd,
    dxo, gates, gd,
    G, XS, DY, W, OWN, SND, RCV, DGU, HID, PM, CC, META, GROW, GS, GR, GT, GX,
    locsem, fs, fr, hs, hr, rfs, rfr, rhs, rhr, wl, ws, wr, ms, mr,
    es, er, ts, tr, gs1, gr1, gs2, gr2, ol, osnd, orcv, ready,
):
    dp = lax.axis_index("dp")
    ex = lax.axis_index("expert")
    pos = [ex % 4, dp // 2, ex // 4]
    core = dp % 2

    def dev(q, c):
        return (q[1] * 2 + c, q[2] * 4 + q[0])

    def shift(q, a, n):
        q = list(q)
        q[a] = (q[a] + n) % 4
        return q

    def blk(q):
        return (q[2] * 4 + q[0]) * 4 + q[1]

    nbr = [(dev(shift(pos, a, 1), core), dev(shift(pos, a, 3), core)) for a in range(3)]
    partner = (pos[1] * 2 + 1 - core, ex)
    me = blk(pos)
    bar = pltpu.get_barrier_semaphore()
    for i in range(1, 16):
        pl.semaphore_signal(bar, inc=1, device_id=(dp, (ex + i) % 16), device_id_type=MESH)
    for i in range(1, 8):
        pl.semaphore_signal(bar, inc=1, device_id=((dp + i) % 8, ex), device_id_type=MESH)

    loc = []
    for c in range(4):
        for w, src in enumerate((tok, gout)):
            loc.append(pltpu.make_async_copy(
                src.at[:, pl.ds(c * 128, 128)], G.at[w, me, pl.ds(c * 128, 128)], locsem.at[2 * c + w]))
    loc.append(pltpu.make_async_copy(meta, META.at[ex], locsem.at[8]))
    for l in loc:
        l.start()
    wcopies = []
    for k, (src, r0, r1) in enumerate(((wg, 0, 384), (wu, 192, 576), (wd, 768, 960))):
        for y in range(4):
            mine = pl.multiple_of(y * 1024 + core * 512, 512)
            theirs = pl.multiple_of(y * 1024 + (1 - core) * 512, 512)
            i = k * 4 + y
            wcopies.append(pltpu.make_async_copy(
                src.at[:, :, pl.ds(mine, 512)], W.at[:, pl.ds(r0, 192), pl.ds(y * 512, 512)], wl.at[i]))
            wcopies.append(pltpu.make_async_remote_copy(
                src.at[:, :, pl.ds(theirs, 512)], W.at[:, pl.ds(r1, 192), pl.ds(y * 512, 512)],
                ws.at[i], wr.at[i], partner, device_id_type=MESH))
    pl.semaphore_wait(bar, 22)
    for l in loc:
        l.wait()

    def origin(s, p, j):
        q = list(pos)
        o = ORDER[p]
        if s >= 1:
            q = shift(q, o[0], j % 4)
        if s == 2:
            q = shift(q, o[1], j // 4)
        return q

    def sem_at(p, s, j, way):
        return (p * 21 + BASE[s] + j) * 2 + way

    def half_rows(p, way):
        r0, n, h = PARTS[p]
        return pl.ds(r0, h) if way == 0 else pl.ds(r0 + h, n - h)

    def part_rows(p):
        return pl.ds(PARTS[p][0], PARTS[p][1])

    def full(v, s, p, j, way):
        i = v * 126 + sem_at(p, s, j, way)
        ref = G.at[v, blk(origin(s, p, j)), part_rows(p)]
        return pltpu.make_async_remote_copy(
            ref, ref, fs.at[i], fr.at[i], nbr[ORDER[p][s]][way], device_id_type=MESH)

    def half(v, s, p, j, way):
        a = ORDER[p][s]
        i = v * 126 + sem_at(p, s, j, way)
        k = blk(shift(origin(s, p, j), a, 3 if way == 0 else 1))
        ref = G.at[v, k, half_rows(p, way)]
        return pltpu.make_async_remote_copy(
            ref, ref, hs.at[i], hr.at[i], nbr[a][way], device_id_type=MESH)

    def each(f):
        for p in range(3):
            for way in range(2):
                f(p, way)

    def odd(f):
        def body(i, c):
            f(1 + 2 * i)
            return c
        lax.fori_loop(0, 2, body, 0)

    def send(v, s, j):
        each(lambda p, w: full(v, s, p, j, w).start())

    def hop(v, s, j):
        def one(p, w):
            full(v, s, p, j, w).wait_recv()
            half(v, s, p, j, w).start()
        each(one)

    def last(v, s, j):
        each(lambda p, w: half(v, s, p, j, w).wait_recv())

    def gather_events(v):
        ev = []
        ev.append(lambda: (send(v, 0, 0), send(v, 1, 0), send(v, 2, 0)))
        ev.append(lambda: (hop(v, 0, 0), odd(lambda a: send(v, 1, a)), odd(lambda a: send(v, 2, group(a, 0)))))
        ev.append(lambda: (hop(v, 1, 0), odd(lambda b: send(v, 2, group(0, b))), hop(v, 2, 0)))
        ev.append(lambda: (last(v, 0, 0), send(v, 1, 2), send(v, 2, group(2, 0))))
        ev.append(lambda: odd(lambda a: (hop(v, 1, a), odd(lambda b: send(v, 2, group(a, b))))))
        ev.append(lambda: (last(v, 1, 0), send(v, 2, group(0, 2))))
        ev.append(lambda: (odd(lambda a: hop(v, 2, group(a, 0))), odd(lambda b: hop(v, 2, group(0, b)))))
        ev.append(lambda: (hop(v, 1, 2), odd(lambda b: send(v, 2, group(2, b)))))
        ev.append(lambda: odd(lambda a: (last(v, 1, a), send(v, 2, group(a, 2)))))
        ev.append(lambda: (hop(v, 2, group(2, 0)), odd(lambda a: odd(lambda b: hop(v, 2, group(a, b))))))
        ev.append(lambda: hop(v, 2, group(0, 2)))
        ev.append(lambda: (last(v, 1, 2), send(v, 2, group(2, 2))))
        ev.append(lambda: (odd(lambda b: hop(v, 2, group(2, b))), odd(lambda a: hop(v, 2, group(a, 2)))))
        ev.append(lambda: hop(v, 2, group(2, 2)))
        return ev

    def gather_rest(v):
        def fin(j, c):
            last(v, 2, j)
            return c
        lax.fori_loop(0, 16, fin, 0)

    def gather_sent(v):
        for s in range(3):
            def fin(j, c, s=s):
                def one(p, w):
                    full(v, s, p, j, w).wait_send()
                    half(v, s, p, j, w).wait_send()
                each(one)
                return c
            lax.fori_loop(0, COUNT[s], fin, 0)

    def meta_copy(i):
        return pltpu.make_async_remote_copy(
            META.at[ex], META.at[ex], ms.at[i], mr.at[i], (dp, (ex + i) % 16), device_id_type=MESH)

    first = (ex * 4).astype(F32)

    def pair_ids(q):
        return jnp.concatenate([META[2 * q, 0:8], META[2 * q + 1, 0:8]], axis=1)

    def prepare():
        sid = META[:, 16, :]
        lr = META[:, 17, :]
        tw = jnp.zeros((16, 128), F32)
        for s in range(SEQS):
            hit = (sid == float(s)).astype(F32)
            total = jnp.sum(jnp.sum(hit * lr, axis=1, keepdims=True), axis=0, keepdims=True)
            count = jnp.sum(jnp.sum(hit, axis=1, keepdims=True), axis=0, keepdims=True)
            wt = adv[s] * jnp.clip(jnp.exp(total / count), clip_low, clip_high)
            tw = tw + hit * wt
        r = lax.broadcasted_iota(jnp.int32, (256, 256), 0)
        t = lax.broadcasted_iota(jnp.int32, (256, 256), 1)
        earlier = ((r < t) & ((r >= 128) == (t >= 128))).astype(F32).astype(BF)
        row = lax.broadcasted_iota(jnp.int32, (2 * CAP, 256), 0)
        lane = lax.broadcasted_iota(jnp.int32, (2 * CAP, 256), 1)
        second = row >= CAP
        same = second == (lane >= 128)
        slot = (row - jnp.where(second, CAP, 0)).astype(F32)
        for q in range(8):
            ids = pair_ids(q)
            gp = jnp.concatenate([META[2 * q, 8:16], META[2 * q + 1, 8:16]], axis=1)
            twq = jnp.concatenate([tw[2 * q:2 * q + 1], tw[2 * q + 1:2 * q + 2]], axis=1)
            hot, cw = [], []
            for n in range(4):
                hit = (ids == first + float(n)).astype(F32)
                hot.append(jnp.sum(hit, axis=0, keepdims=True))
                cw.append(jnp.sum(hit * gp, axis=0, keepdims=True) * twq)
            hots = jnp.concatenate(hot + hot, axis=0)
            rank = jnp.dot(hots.astype(BF), earlier, preferred_element_type=F32)
            for n in range(4):
                sel = same & (rank[n:n + 1] == slot) & (hot[n] > 0.5)
                pick = sel.astype(F32)
                PM[q, n * 48:(n + 1) * 48, :] = pick.astype(BF)
                cc = jnp.sum(pick * cw[n], axis=1, keepdims=True)
                CC[q, n * 48:(n + 1) * 48, :] = jnp.broadcast_to(cc, (48, 128))

    def select(v, q):
        dst = XS if v == 0 else DY
        rows = pl.ds(pl.multiple_of(q * 48, 16), 48)
        pm = PM[q]
        for y in range(4):
            xp = jnp.concatenate([
                jnp.concatenate([G[v, (2 * q + b) * 4 + y, c * 128:(c + 1) * 128, :] for c in range(4)], axis=1)
                for b in range(2)], axis=0)
            r = jnp.dot(pm, xp, preferred_element_type=F32)
            if v == 1:
                r = r * CC[q, :, 0:1]
            r = r.astype(BF)
            for n in range(4):
                dst[n, rows, y * 512:(y + 1) * 512] = r[n * 48:(n + 1) * 48]

    def loop(lo, hi, f):
        def body(i, c):
            f(i)
            return c
        lax.fori_loop(lo, hi, body, 0)

    def swap_gu(n):
        return pltpu.make_async_remote_copy(
            SND.at[n, pl.ds(0, 384)], RCV.at[n, pl.ds(0, 384)], es.at[n], er.at[n], partner, device_id_type=MESH)

    def swap_z(n):
        return pltpu.make_async_remote_copy(
            SND.at[n, pl.ds(384, 192)], RCV.at[n, pl.ds(384, 192)], es.at[4 + n], er.at[4 + n], partner,
            device_id_type=MESH)

    def gate_up(n):
        x = XS[n]
        OWN[n, 0:384] = lax.dot_general(W[n, 0:384], x, NT, preferred_element_type=F32)
        SND[n, 0:384] = lax.dot_general(W[n, 384:768], x, NT, preferred_element_type=F32).astype(BF)
        swap_gu(n).start()

    def down(n):
        z = lax.dot_general(W[n, 768:1152], DY[n], NT, preferred_element_type=F32)
        OWN[n, 384:576] = z[0:192]
        SND[n, 384:576] = z[192:384].astype(BF)
        swap_z(n).start()

    def swap_d(n):
        return pltpu.make_async_remote_copy(
            DGU.at[n, pl.ds(0, 384)], DGU.at[n, pl.ds(384, 384)], ts.at[n], tr.at[n], partner, device_id_type=MESH)

    def swap_h(n):
        return pltpu.make_async_remote_copy(
            HID.at[n, pl.ds(0, 192)], HID.at[n, pl.ds(192, 192)], ts.at[4 + n], tr.at[4 + n], partner,
            device_id_type=MESH)

    def middle(n):
        swap_gu(n).wait_recv()
        swap_z(n).wait_recv()
        g = OWN[n, 0:192] + RCV[n, 0:192].astype(F32)
        u = OWN[n, 192:384] + RCV[n, 192:384].astype(F32)
        z = OWN[n, 384:576] + RCV[n, 384:576].astype(F32)
        sg = jax.nn.sigmoid(g)
        gsg = g * sg
        h = (gsg * u).astype(BF)
        DGU[n, 0:192] = (z * u * sg * (1.0 + g * (1.0 - sg))).astype(BF)
        DGU[n, 192:384] = (z * gsg).astype(BF)
        HID[n, 0:192] = h
        GROW[n] = jnp.broadcast_to(jnp.sum(h.astype(F32) * z, axis=0, keepdims=True), (8, 384))
        swap_d(n).start()
        swap_h(n).start()

    def grad_x(n):
        swap_d(n).wait_recv()
        d = DGU[n].T
        for y in range(4):
            cols = slice(y * 512, (y + 1) * 512)
            XS[n, :, cols] = jnp.dot(d, W[n, 0:768, cols], preferred_element_type=F32).astype(BF)

    def scatter(q):
        rows = pl.ds(pl.multiple_of(q * 48, 16), 48)
        pt = PM[q].T
        for y in range(4):
            part = jnp.concatenate([XS[n, rows, y * 512:(y + 1) * 512] for n in range(4)], axis=0)
            r = jnp.dot(pt, part, preferred_element_type=F32).astype(BF)
            for b in range(2):
                for c in range(4):
                    G[0, (2 * q + b) * 4 + y, c * 128:(c + 1) * 128, :] = (
                        r[b * 128:(b + 1) * 128, c * 128:(c + 1) * 128])

    def out_local(n, y):
        cols = pl.multiple_of(y * 1024 + core * 512, 512)
        return pltpu.make_async_copy(
            XS.at[n, pl.ds(0, 192), pl.ds(y * 512, 512)], gd.at[n, :, pl.ds(cols, 512)], ol.at[n * 4 + y])

    def out_remote(n, y):
        cols = pl.multiple_of(y * 1024 + core * 512, 512)
        return pltpu.make_async_remote_copy(
            XS.at[n, pl.ds(192, 192), pl.ds(y * 512, 512)], gd.at[n, :, pl.ds(cols, 512)],
            osnd.at[n * 4 + y], orcv.at[n * 4 + y], partner, device_id_type=MESH)

    def grad_down(n):
        swap_h(n).wait_recv()
        h = HID[n]
        for y in range(4):
            cols = slice(y * 512, (y + 1) * 512)
            XS[n, :, cols] = jnp.dot(h, DY[n, :, cols], preferred_element_type=F32).astype(BF)
            out_local(n, y).start()
            out_remote(n, y).start()

    def gate_tokens():
        lane = lax.broadcasted_iota(jnp.int32, (8, 192), 1)
        row = lax.broadcasted_iota(jnp.int32, (8, 192), 0)
        own = (lane >= row * 48) & (lane < row * 48 + 48)
        for q in range(8):
            vals = jnp.concatenate([GROW[n, 0:1, q * 48:(q + 1) * 48] for n in range(4)], axis=1)
            a = jnp.where(own, vals, 0.0)
            gt = jnp.dot(a, PM[q].astype(F32), precision=lax.Precision.HIGHEST, preferred_element_type=F32)
            ids = pair_ids(q)
            r = jnp.zeros((8, 256), F32)
            for n in range(4):
                r = r + jnp.where(ids == first + float(n), gt[n:n + 1], 0.0)
            GS[2 * q] = r[:, 0:128]
            GS[2 * q + 1] = r[:, 128:256]

    def gate_one(i):
        e = (ex + i) % 16
        return pltpu.make_async_remote_copy(
            GS.at[e], GR.at[i], gs1.at[i], gr1.at[i], (dp, e), device_id_type=MESH)

    def gate_two(i):
        return pltpu.make_async_remote_copy(
            GT, GX.at[i], gs2.at[i], gr2.at[i], ((dp + i) % 8, ex), device_id_type=MESH)

    def rhalf(s, p, j, way):
        a = ORDER[p][s]
        i = sem_at(p, s, j, way)
        k = blk(shift(origin(s, p, j), a, 2))
        rows = half_rows(p, way)
        return pltpu.make_async_remote_copy(
            G.at[0, k, rows], G.at[1, BASE[s] + j, rows], rhs.at[i], rhr.at[i], nbr[a][way], device_id_type=MESH)

    def rfull(s, p, j, way):
        a = ORDER[p][s]
        i = sem_at(p, s, j, way)
        k = blk(shift(origin(s, p, j), a, 1 if way == 0 else 3))
        rows = part_rows(p)
        return pltpu.make_async_remote_copy(
            G.at[0, k, rows], G.at[1, 21 + (BASE[s] + j) * 2 + way, rows], rfs.at[i], rfr.at[i], nbr[a][way],
            device_id_type=MESH)

    def r_start(s, j):
        each(lambda p, w: rhalf(s, p, j, w).start())

    def r_mid(s, j):
        def one(p, way):
            rhalf(s, p, j, way).wait_recv()
            k = blk(shift(origin(s, p, j), ORDER[p][s], 1 if way == 0 else 3))
            rows = half_rows(p, way)
            G[0, k, rows] = (G[0, k, rows].astype(F32) + G[1, BASE[s] + j, rows].astype(F32)).astype(BF)
            rfull(s, p, j, way).start()
        each(one)

    def r_end(s, j):
        for p in range(3):
            for way in range(2):
                rfull(s, p, j, way).wait_recv()
            k = blk(origin(s, p, j))
            rows = part_rows(p)
            f = 21 + (BASE[s] + j) * 2
            G[0, k, rows] = (G[0, k, rows].astype(F32) + (
                G[1, f, rows].astype(F32) + G[1, f + 1, rows].astype(F32))).astype(BF)

    def r_sent():
        for s in range(3):
            def fin(j, c, s=s):
                def one(p, w):
                    rhalf(s, p, j, w).wait_send()
                    rfull(s, p, j, w).wait_send()
                each(one)
                return c
            lax.fori_loop(0, COUNT[s], fin, 0)

    far = (2, 3, 1, 0)
    for i in range(1, 16):
        meta_copy(i).start()
    ev0 = gather_events(0)
    ev0[0]()
    for c in wcopies:
        c.start()
    for i in range(1, 16):
        meta_copy(i).wait()
    ev0[1]()
    ev0[2]()
    prepare()
    for e in ev0[3:]:
        e()
    ev1 = gather_events(1)
    ev1[0]()
    gather_rest(0)
    ev1[1]()
    ev1[2]()
    ev1[3]()
    loop(0, 4, lambda q: select(0, q))
    ev1[4]()
    ev1[5]()
    ev1[6]()
    loop(4, 8, lambda q: select(0, q))
    for c in wcopies:
        c.wait()
    ev1[7]()
    ev1[8]()
    ev1[9]()
    loop(0, 2, gate_up)
    for e in ev1[10:]:
        e()
    loop(2, 4, gate_up)
    gather_rest(1)
    loop(0, 8, lambda q: select(1, q))
    gather_sent(0)
    gather_sent(1)
    for a in range(3):
        for n in nbr[a]:
            pl.semaphore_signal(ready, inc=1, device_id=n, device_id_type=MESH)
    loop(0, 4, down)
    loop(0, 4, middle)
    loop(0, 4, grad_x)
    loop(0, 8, scatter)
    pl.semaphore_wait(ready, 6)
    for b in far:
        loop(0, 4, lambda a, b=b: r_start(2, group((a + 2) % 4, b)))
    gate_tokens()
    for i in range(1, 16):
        gate_one(i).start()
    for b in far:
        loop(0, 4, lambda a, b=b: r_mid(2, group((a + 2) % 4, b)))
    loop(0, 4, grad_down)
    for i in range(1, 16):
        gate_one(i).wait()
    acc = GS[ex]
    for i in range(1, 16):
        acc = acc + GR[i]
    GT[...] = acc
    for i in range(1, 8):
        gate_two(i).start()
    for a in far:
        r_end(2, group(a, 2))
        r_start(1, a)
    for a in far:
        r_end(2, group(a, 1))
        r_end(2, group(a, 3))
        r_mid(1, a)
    r_end(2, group(2, 0))
    r_end(1, 2)
    r_start(0, 0)
    for a in (1, 3):
        r_end(2, group(a, 0))
        r_end(1, a)
    r_mid(0, 0)
    r_end(2, 0)
    r_end(1, 0)
    r_end(0, 0)
    for c in range(4):
        dxo[:, c * 128:(c + 1) * 128] = G[0, me, c * 128:(c + 1) * 128, :]
    for i in range(1, 8):
        gate_two(i).wait()
    acc = GT[...]
    for i in range(1, 8):
        acc = acc + GX[i]
    gates[...] = acc
    r_sent()

    def finish(n):
        swap_gu(n).wait_send()
        swap_z(n).wait_send()
        swap_d(n).wait_send()
        swap_h(n).wait_send()
        for y in range(4):
            out_local(n, y).wait()
            out_remote(n, y).wait()
    loop(0, 4, finish)


def on_device(
    tokens, grad_out, expert_ids, gate_probs, seq_ids, log_ratio, advantages, w_gate, w_up, w_down
):
    meta = jnp.concatenate([
        expert_ids.astype(F32).T, gate_probs.T, seq_ids.astype(F32)[None], log_ratio[None],
        jnp.zeros((6, 128), F32)], axis=0)
    vmem = pl.BlockSpec(memory_space=pltpu.VMEM)
    hbm = pl.BlockSpec(memory_space=pl.ANY)
    dma = lambda n: pltpu.SemaphoreType.DMA((n,))
    dx, gates, gd = pl.pallas_call(
        step_kernel,
        out_shape=(
            jax.ShapeDtypeStruct((128, 512), BF),
            jax.ShapeDtypeStruct((8, 128), F32),
            jax.ShapeDtypeStruct((4, 192, 4096), BF),
        ),
        in_specs=[pl.BlockSpec(memory_space=pltpu.SMEM), vmem, vmem, vmem, hbm, hbm, hbm],
        out_specs=(vmem, vmem, hbm),
        scratch_shapes=[
            pltpu.VMEM((2, 64, 512, 128), BF),
            pltpu.VMEM((4, 384, 2048), BF),
            pltpu.VMEM((4, 384, 2048), BF),
            pltpu.VMEM((4, 1152, 2048), BF),
            pltpu.VMEM((4, 576, 384), F32),
            pltpu.VMEM((4, 576, 384), BF),
            pltpu.VMEM((4, 576, 384), BF),
            pltpu.VMEM((4, 768, 384), BF),
            pltpu.VMEM((4, 384, 384), BF),
            pltpu.VMEM((8, 192, 256), BF),
            pltpu.VMEM((8, 192, 128), F32),
            pltpu.VMEM((16, 24, 128), F32),
            pltpu.VMEM((4, 8, 384), F32),
            pltpu.VMEM((16, 8, 128), F32),
            pltpu.VMEM((16, 8, 128), F32),
            pltpu.VMEM((8, 128), F32),
            pltpu.VMEM((8, 8, 128), F32),
            dma(9), dma(252), dma(252), dma(252), dma(252), dma(126), dma(126), dma(126), dma(126),
            dma(12), dma(12), dma(12), dma(16), dma(16),
            dma(8), dma(8), dma(8), dma(8), dma(16), dma(16), dma(8), dma(8), dma(16), dma(16), dma(16),
            pltpu.SemaphoreType.REGULAR,
        ],
        compiler_params=pltpu.CompilerParams(
            collective_id=0, has_side_effects=True, vmem_limit_bytes=67043328),
        name="expert_step",
    )(advantages, tokens, grad_out, meta, w_gate, w_up, w_down)
    return dx, gates.T / gate_probs, gd


def solution(mesh):
    return jax.shard_map(
        on_device,
        mesh=mesh,
        in_specs=(
            P("expert", "dp"),
            P("expert", "dp"),
            P("expert", None),
            P("expert", None),
            P("expert"),
            P("expert"),
            P(),
            P("expert", "dp", None),
            P("expert", "dp", None),
            P("expert", "dp", None),
        ),
        out_specs=(P("expert", "dp"), P("expert", None), P("expert", "dp", None)),
        check_vma=False,
    )
```

time: 736 us -> 166 us (0.23)
  waiting for transfers between devices: 249 us -> 0 us
  blocking collectives: 246 us -> 0 us
  Pallas kernels: 0 us -> 151 us
  local copies, waits for them, and re-layouts: 104 us -> 11 us
  matrix products: 69.6 us -> 0 us
  starting transfers between devices: 22.9 us -> 0 us
  other arithmetic: 23.8 us -> 2.64 us
  between operations: 14.2 us -> 0.64 us
    psum x2 -> x0, blocking collectives: 236 us -> none  [the longest x1 212 us: on_device(): sums, counts = lax.psum((local_sums, local_counts), 'expert')]
    pallas_call x0 -> x1, Pallas kernels: none -> 151 us  [on_device(): pl.pallas_call(step_kernel, out_shape=(jax.ShapeDtypeStruct((128, 512), B...]
    all_to_all x4 -> x0, waiting for transfers between devices: 148 us -> none  [the longest x1 126 us: on_device(): lax.all_to_all(place(full_x), 'expert', split_axis=0, concat_axis=0, tile...]
    dot_general x8 -> x0, matrix products: 69.6 us -> none  [the longest x1 15.9 us: on_device(): jnp.einsum('snrf,nfd->snrd', du, w_up, preferred_element_type=jnp.float32)]
    reduce_scatter x1 -> x0, waiting for transfers between devices: 66.9 us -> none  [on_device(): lax.psum_scatter(part.astype(jnp.bfloat16), 'dp', scatter_dimension=3, ti...]
    scatter x3 -> x0, local copies, waits for them, and re-layouts: 54.1 us -> none  [the longest x2 49.8 us: place(): buffer.at[dest].set(rows[token_of])]
    gather x4 -> x0, local copies, waits for them, and re-layouts: 43.9 us -> none  [the longest x2 32.9 us: place(): rows[token_of]]
    all_gather x2 -> x0, waiting for transfers between devices: 32.5 us -> none  [the longest x1 25.3 us: on_device(): lax.all_gather(grad_out, 'dp', axis=1, tiled=True)]
  transfers between devices with their start and end apart: 7 -> 0, of which waited for: 6 -> 0; matrix products, arithmetic and copies ran while one was open for 12% -> 0% of each run, Pallas kernels for 0% -> 0%
where the time goes in v1:
time: 166 us; the launch traced here: 165 us
  Pallas kernels  151 us (91%)
  local copies, waits for them, and re-layouts  11 us (7%)
  other arithmetic  2.64 us (2%)
    pallas_call x1, Pallas kernels, on_device(): pl.pallas_call(step_kernel, out_shape=(jax.ShapeDtypeStruct((128, 512), B...  151 us
    unnamed x2, local copies, waits for them, and re-layouts  7.85 us

profile of v1, /device:TPU:0, one launch (start us, length us, event | category | flops | bytes accessed | tf_op | source)
XLA Modules:
  0.0 165.5 jit_solution(4584517031492621237)
XLA Ops:
  0.6 0.7 convert_bitcast_fusion.1
  1.3 0.7 convert_bitcast_fusion
  2.0 3.1 %concatenate.3.meta = f32[24,128]{1,0:T(8,128)} concatenate(f32[8,128]{1,0:T(8,128)S(1)} %convert_bitcast_fusion, f32[8,128]{1,0:T(8,128)} %bitcast.8, f32[1,128]{1,0:T(1,128)S(1)} %convert_bitcast_fusion.1, f32[1,128]{1,0:T(1,128)} %bitcast.9, f32[6,128]{1,0:T(8,128)S(1)} %broadcast_in_dim.11), dimensions={0} | concatenate | bytes 24576 | tf_op jit(solution)/shard_map/concatenate | solution.py:500
  5.1 151.2 %expert_step.1 = (bf16[128,512]{1,0:T(8,128)(2,1)}, f32[8,128]{1,0:T(8,128)}, bf16[4,192,4096]{2,1,0:T(8,128)(2,1)}) custom-call(f32[8]{0:T(128)} %adv.1, bf16[128,512]{1,0:T(8,128)(2,1)} %tok.1, bf16[128,512]{1,0:T(8,128)(2,1)} %gout.1, f32[24,128]{1,0:T(8,128)} %concatenate.3.meta, bf16[4,192,4096]{2,1,0:T(8,128)(2,1)} %wg.1, bf16[4,192,4096]{2,1,0:T(8,128)(2,1)} %wu.1, ...), custom_call_target="tpu_custom_call" | custom-call | tf_op jit(solution)/shard_map/expert_step/pallas_call | solution.py:506
  156.3 1.3 bitcast_divide_fusion
  157.6 1.6 copy.15
  159.2 6.3 %copy.16 = bf16[4,192,4096]{2,1,0:T(8,128)(2,1)} copy(bf16[4,192,4096]{2,1,0:T(8,128)(2,1)} %get-tuple-element.14) | data formatting | bytes 12582912
  (1 shorter events, 0.0 us)

commit v2 on v1

v2 whole, which is shorter than its diff:
```python
import jax
import jax.numpy as jnp
from jax import lax
from jax.experimental import pallas as pl
from jax.experimental.pallas import tpu as pltpu
from jax.sharding import PartitionSpec as P

SEQS = 8
TOP = 8
CAP = 24
clip_low = 0.9
clip_high = 1.1

MESH = pl.DeviceIdType.MESH
BF = jnp.bfloat16
F32 = jnp.float32
PARTS = ((0, 176, 96), (176, 176, 80), (352, 160, 80))
ORDER = ((0, 1, 2), (1, 2, 0), (2, 0, 1))
BASE = (0, 1, 5)
COUNT = (1, 4, 16)
NT = (((1,), (1,)), ((), ()))
TN = (((0,), (0,)), ((), ()))


def group(a, b):
    return b * 4 + a


def step_kernel(
    adv, tok, gout, idt, gpt, seq, ratio, wg, wu, wd,
    dxo, gates, gd,
    G, XS, DY, W, OWN, SND, RCV, DT, HID, PM, PT, CC, META, GROW, GS, GR, GT, GX,
    locsem, sent, fr, hr, wl, ws, wr, ms, mr,
    es, er, ts, tr, th, gs1, gr1, gs2, gr2, ol, osnd, orcv, ready,
):
    dp = lax.axis_index("dp")
    ex = lax.axis_index("expert")
    pos = [ex % 4, dp // 2, ex // 4]
    core = dp % 2

    def dev(q, c):
        return (q[1] * 2 + c, q[2] * 4 + q[0])

    def shift(q, a, n):
        q = list(q)
        q[a] = (q[a] + n) % 4
        return q

    def blk(q):
        return (q[2] * 4 + q[0]) * 4 + q[1]

    nbr = [(dev(shift(pos, a, 1), core), dev(shift(pos, a, 3), core)) for a in range(3)]
    partner = (pos[1] * 2 + 1 - core, ex)
    me = blk(pos)
    bar = pltpu.get_barrier_semaphore()
    for i in range(1, 16):
        pl.semaphore_signal(bar, inc=1, device_id=(dp, (ex + i) % 16), device_id_type=MESH)
    for i in range(1, 8):
        pl.semaphore_signal(bar, inc=1, device_id=((dp + i) % 8, ex), device_id_type=MESH)

    def settle(ref, sem):
        pltpu.make_async_copy(ref, ref, sem).wait()

    for c in range(4):
        for w, src in enumerate((tok, gout)):
            pltpu.make_async_copy(
                src.at[:, pl.ds(c * 128, 128)], G.at[w, me, pl.ds(c * 128, 128)], locsem.at[w]).start()
    META[ex, 0:8, :] = idt[...].astype(F32)
    META[ex, 8:16, :] = gpt[...]
    META[ex, 16:17, :] = seq[...].astype(F32)
    META[ex, 17:18, :] = ratio[...]

    def fetch_weights():
        for k, (src, r0, r1) in enumerate(((wg, 0, 384), (wu, 192, 576), (wd, 768, 960))):
            for y in range(4):
                mine = pl.multiple_of(y * 1024 + core * 512, 512)
                theirs = pl.multiple_of(y * 1024 + (1 - core) * 512, 512)
                pltpu.make_async_copy(
                    src.at[:, :, pl.ds(mine, 512)], W.at[:, pl.ds(r0, 192), pl.ds(y * 512, 512)], wl.at[0]).start()
                pltpu.make_async_remote_copy(
                    src.at[:, :, pl.ds(theirs, 512)], W.at[:, pl.ds(r1, 192), pl.ds(y * 512, 512)],
                    ws.at[0], wr.at[0], partner, device_id_type=MESH).start()

    def settle_weights():
        for sem in (wl, ws, wr):
            settle(W.at[:, pl.ds(0, 576)], sem.at[0])

    pl.semaphore_wait(bar, 22)
    for w in range(2):
        settle(G.at[w, me], locsem.at[w])

    def origin(s, p, j):
        q = list(pos)
        o = ORDER[p]
        if s >= 1:
            q = shift(q, o[0], j % 4)
        if s == 2:
            q = shift(q, o[1], j // 4)
        return q

    def slot(s, k):
        return (0, 1, 5)[s] + k

    def full_sem(v, p, way, k):
        return ((v * 3 + p) * 2 + way) * 9 + k

    def half_sem(v, p, way, k):
        return ((v * 3 + p) * 2 + way) * 6 + k

    def sent_sem(v, p, way):
        return (v * 3 + p) * 2 + way

    def half_rows(p, way):
        r0, n, h = PARTS[p]
        return pl.ds(r0, h) if way == 0 else pl.ds(r0 + h, n - h)

    def part_rows(p):
        return pl.ds(PARTS[p][0], PARTS[p][1])

    def full(v, s, p, j, way):
        ref = G.at[v, blk(origin(s, p, j)), part_rows(p)]
        k = slot(s, j // 4 if s == 2 else j)
        return pltpu.make_async_remote_copy(
            ref, ref, sent.at[sent_sem(v, p, way)], fr.at[full_sem(v, p, way, k)], nbr[ORDER[p][s]][way],
            device_id_type=MESH)

    def half(v, s, p, j, way):
        a = ORDER[p][s]
        b = blk(shift(origin(s, p, j), a, 3 if way == 0 else 1))
        ref = G.at[v, b, half_rows(p, way)]
        k = 5 if s == 2 else slot(s, j)
        return pltpu.make_async_remote_copy(
            ref, ref, sent.at[sent_sem(v, p, way)], hr.at[half_sem(v, p, way, k)], nbr[a][way],
            device_id_type=MESH)

    def each(f):
        for p in range(3):
            for way in range(2):
                f(p, way)

    def odd(f):
        def body(i, c):
            f(1 + 2 * i)
            return c
        lax.fori_loop(0, 2, body, 0)

    def loop(lo, hi, f):
        def body(i, c):
            f(i)
            return c
        lax.fori_loop(lo, hi, body, 0)

    def send(v, s, j):
        each(lambda p, w: full(v, s, p, j, w).start())

    def hop(v, s, j):
        def one(p, w):
            full(v, s, p, j, w).wait_recv()
            half(v, s, p, j, w).start()
        each(one)

    def hop_bundle(v, b):
        for p in range(3):
            for w in range(2):
                settle(G.at[v, pl.ds(0, 4), part_rows(p)], fr.at[full_sem(v, p, w, slot(2, b))])
                loop(0, 4, lambda a, p=p, w=w: half(v, 2, p, group(a, b), w).start())

    def last(v, s, j):
        each(lambda p, w: half(v, s, p, j, w).wait_recv())

    def gather_events(v):
        ev = []
        ev.append(lambda: (send(v, 0, 0), send(v, 1, 0), send(v, 2, 0)))
        ev.append(lambda: (hop(v, 0, 0), odd(lambda a: send(v, 1, a)), odd(lambda a: send(v, 2, group(a, 0)))))
        ev.append(lambda: (hop(v, 1, 0), odd(lambda b: send(v, 2, group(0, b)))))
        ev.append(lambda: (last(v, 0, 0), send(v, 1, 2), send(v, 2, group(2, 0))))
        ev.append(lambda: odd(lambda a: (hop(v, 1, a), odd(lambda b: send(v, 2, group(a, b))))))
        ev.append(lambda: (last(v, 1, 0), send(v, 2, group(0, 2))))
        ev.append(lambda: hop_bundle(v, 0))
        ev.append(lambda: (hop(v, 1, 2), odd(lambda b: send(v, 2, group(2, b)))))
        ev.append(lambda: odd(lambda a: (last(v, 1, a), send(v, 2, group(a, 2)))))
        ev.append(lambda: (last(v, 1, 2), send(v, 2, group(2, 2))))
        ev.append(lambda: odd(lambda b: hop_bundle(v, b)))
        ev.append(lambda: hop_bundle(v, 2))
        return ev

    def gather_rest(v):
        def one(p, w):
            h = PARTS[p][2] if w == 0 else PARTS[p][1] - PARTS[p][2]
            settle(G.at[v, pl.ds(0, 16), pl.ds(0, h)], hr.at[half_sem(v, p, w, 5)])
        each(one)

    def all_sent(v):
        def one(p, w):
            h = PARTS[p][2] if w == 0 else PARTS[p][1] - PARTS[p][2]
            settle(G.at[v, pl.ds(0, 21), pl.ds(0, PARTS[p][1] + h)], sent.at[sent_sem(v, p, w)])
        each(one)

    def meta_copy(i):
        return pltpu.make_async_remote_copy(
            META.at[ex], META.at[ex], ms.at[0], mr.at[0], (dp, (ex + i) % 16), device_id_type=MESH)

    first = (ex * 4).astype(F32)

    def pair_ids(q):
        return jnp.concatenate([META[2 * q, 0:8], META[2 * q + 1, 0:8]], axis=1)

    def prepare():
        sid = META[:, 16, :]
        lr = META[:, 17, :]
        tw = jnp.zeros((16, 128), F32)
        for s in range(SEQS):
            hit = (sid == float(s)).astype(F32)
            total = jnp.sum(jnp.sum(hit * lr, axis=1, keepdims=True), axis=0, keepdims=True)
            count = jnp.sum(jnp.sum(hit, axis=1, keepdims=True), axis=0, keepdims=True)
            wt = adv[s] * jnp.clip(jnp.exp(total / count), clip_low, clip_high)
            tw = tw + hit * wt
        r = lax.broadcasted_iota(jnp.int32, (256, 256), 0)
        t = lax.broadcasted_iota(jnp.int32, (256, 256), 1)
        earlier = ((r < t) & ((r >= 128) == (t >= 128))).astype(F32).astype(BF)
        row = lax.broadcasted_iota(jnp.int32, (2 * CAP, 256), 0)
        lane = lax.broadcasted_iota(jnp.int32, (2 * CAP, 256), 1)
        second = row >= CAP
        same = second == (lane >= 128)
        slot = (row - jnp.where(second, CAP, 0)).astype(F32)
        for q in range(8):
            ids = pair_ids(q)
            gp = jnp.concatenate([META[2 * q, 8:16], META[2 * q + 1, 8:16]], axis=1)
            twq = jnp.concatenate([tw[2 * q:2 * q + 1], tw[2 * q + 1:2 * q + 2]], axis=1)
            hot, cw = [], []
            for n in range(4):
                hit = (ids == first + float(n)).astype(F32)
                hot.append(jnp.sum(hit, axis=0, keepdims=True))
                cw.append(jnp.sum(hit * gp, axis=0, keepdims=True) * twq)
            hots = jnp.concatenate(hot + hot, axis=0)
            rank = jnp.dot(hots.astype(BF), earlier, preferred_element_type=F32)
            for n in range(4):
                sel = same & (rank[n:n + 1] == slot) & (hot[n] > 0.5)
                pick = sel.astype(F32)
                PM[q, n * 48:(n + 1) * 48, :] = pick.astype(BF)
                cc = jnp.sum(pick * cw[n], axis=1, keepdims=True)
                CC[q, n * 48:(n + 1) * 48, :] = jnp.broadcast_to(cc, (48, 128))
            PT[q] = PM[q].T

    def select(v, q):
        dst = XS if v == 0 else DY
        rows = pl.ds(pl.multiple_of(q * 48, 16), 48)
        pm = PM[q]
        for y in range(4):
            xp = jnp.concatenate([
                jnp.concatenate([G[v, (2 * q + b) * 4 + y, c * 128:(c + 1) * 128, :] for c in range(4)], axis=1)
                for b in range(2)], axis=0)
            r = jnp.dot(pm, xp, preferred_element_type=F32)
            if v == 1:
                r = r * CC[q, :, 0:1]
            r = r.astype(BF)
            for n in range(4):
                dst[n, rows, y * 512:(y + 1) * 512] = r[n * 48:(n + 1) * 48]

    def swap_gu(n):
        return pltpu.make_async_remote_copy(
            SND.at[n, pl.ds(0, 384)], RCV.at[n, pl.ds(0, 384)], es.at[0], er.at[n], partner, device_id_type=MESH)

    def swap_z(n):
        return pltpu.make_async_remote_copy(
            SND.at[n, pl.ds(384, 192)], RCV.at[n, pl.ds(384, 192)], es.at[0], er.at[4 + n], partner,
            device_id_type=MESH)

    def gate_up(n):
        x = XS[n]
        OWN[n, 0:384] = lax.dot_general(W[n, 0:384], x, NT, preferred_element_type=F32)
        SND[n, 0:384] = lax.dot_general(W[n, 384:768], x, NT, preferred_element_type=F32).astype(BF)
        swap_gu(n).start()

    def down(n):
        z = lax.dot_general(W[n, 768:1152], DY[n], NT, preferred_element_type=F32)
        OWN[n, 384:576] = z[0:192]
        SND[n, 384:576] = z[192:384].astype(BF)
        swap_z(n).start()

    def swap_d(n):
        return pltpu.make_async_remote_copy(
            DT.at[n, :, pl.ds(0, 384)], DT.at[n, :, pl.ds(384, 384)], ts.at[0], tr.at[n], partner,
            device_id_type=MESH)

    def swap_h(n):
        return pltpu.make_async_remote_copy(
            HID.at[n, pl.ds(0, 192)], HID.at[n, pl.ds(192, 192)], ts.at[1], th.at[0], partner,
            device_id_type=MESH)

    def hidden(n):
        swap_gu(n).wait_recv()
        g = OWN[n, 0:192] + RCV[n, 0:192].astype(F32)
        u = OWN[n, 192:384] + RCV[n, 192:384].astype(F32)
        sg = jax.nn.sigmoid(g)
        gsg = g * sg
        HID[n, 0:192] = (gsg * u).astype(BF)
        OWN[n, 0:192] = u * sg * (1.0 + g * (1.0 - sg))
        OWN[n, 192:384] = gsg
        swap_h(n).start()

    def middle(n):
        swap_z(n).wait_recv()
        z = OWN[n, 384:576] + RCV[n, 384:576].astype(F32)
        d = jnp.concatenate([OWN[n, 0:192] * z, OWN[n, 192:384] * z], axis=0).astype(BF)
        DT[n, :, 0:384] = d.T
        swap_d(n).start()
        GROW[n] = jnp.broadcast_to(jnp.sum(HID[n, 0:192].astype(F32) * z, axis=0, keepdims=True), (8, 384))

    def grad_x(n, y):
        cols = pl.ds(pl.multiple_of(y * 512, 512), 512)
        XS[n, :, cols] = jnp.dot(DT[n], W[n, 0:768, cols], preferred_element_type=F32).astype(BF)

    def scatter(q, y):
        rows = pl.ds(pl.multiple_of(q * 48, 16), 48)
        cols = pl.ds(pl.multiple_of(y * 512, 512), 512)
        part = jnp.concatenate([XS[n, rows, cols] for n in range(4)], axis=0)
        r = jnp.dot(PT[q], part, preferred_element_type=F32).astype(BF)
        for b in range(2):
            for c in range(4):
                G[0, (2 * q + b) * 4 + y, c * 128:(c + 1) * 128, :] = (
                    r[b * 128:(b + 1) * 128, c * 128:(c + 1) * 128])

    def out_local(n, y):
        cols = pl.multiple_of(y * 1024 + core * 512, 512)
        return pltpu.make_async_copy(
            XS.at[n, pl.ds(0, 192), pl.ds(y * 512, 512)], gd.at[n, :, pl.ds(cols, 512)], ol.at[0])

    def out_remote(n, y):
        cols = pl.multiple_of(y * 1024 + core * 512, 512)
        return pltpu.make_async_remote_copy(
            XS.at[n, pl.ds(192, 192), pl.ds(y * 512, 512)], gd.at[n, :, pl.ds(cols, 512)],
            osnd.at[0], orcv.at[0], partner, device_id_type=MESH)

    def grad_down(n):
        h = HID[n]
        for y in range(4):
            cols = slice(y * 512, (y + 1) * 512)
            XS[n, :, cols] = jnp.dot(h, DY[n, :, cols], preferred_element_type=F32).astype(BF)
            out_local(n, y).start()
            out_remote(n, y).start()

    def gate_tokens():
        lane = lax.broadcasted_iota(jnp.int32, (8, 192), 1)
        row = lax.broadcasted_iota(jnp.int32, (8, 192), 0)
        own = (lane >= row * 48) & (lane < row * 48 + 48)
        for q in range(8):
            vals = jnp.concatenate([GROW[n, 0:1, q * 48:(q + 1) * 48] for n in range(4)], axis=1)
            a = jnp.where(own, vals, 0.0)
            gt = jnp.dot(a, PM[q].astype(F32), precision=lax.Precision.HIGHEST, preferred_element_type=F32)
            ids = pair_ids(q)
            r = jnp.zeros((8, 256), F32)
            for n in range(4):
                r = r + jnp.where(ids == first + float(n), gt[n:n + 1], 0.0)
            GS[2 * q] = r[:, 0:128]
            GS[2 * q + 1] = r[:, 128:256]

    def gate_one(i):
        e = (ex + i) % 16
        return pltpu.make_async_remote_copy(
            GS.at[e], GR.at[i], gs1.at[0], gr1.at[0], (dp, e), device_id_type=MESH)

    def gate_two(i):
        return pltpu.make_async_remote_copy(
            GT, GX.at[i], gs2.at[0], gr2.at[0], ((dp + i) % 8, ex), device_id_type=MESH)

    def member(p, k, i):
        return group(k, i) if p == 1 else group(i, k)

    def rslot(s, p, j):
        if s < 2:
            return slot(s, j)
        return slot(2, j % 4 if p == 1 else j // 4)

    def rhalf(s, p, j, way):
        a = ORDER[p][s]
        k = blk(shift(origin(s, p, j), a, 2))
        rows = half_rows(p, way)
        return pltpu.make_async_remote_copy(
            G.at[0, k, rows], G.at[1, BASE[s] + j, rows], sent.at[sent_sem(0, p, way)],
            fr.at[full_sem(0, p, way, rslot(s, p, j))], nbr[a][way], device_id_type=MESH)

    def rfull(s, p, j, way):
        a = ORDER[p][s]
        k = blk(shift(origin(s, p, j), a, 1 if way == 0 else 3))
        rows = part_rows(p)
        return pltpu.make_async_remote_copy(
            G.at[0, k, rows], G.at[1, 21 + (BASE[s] + j) * 2 + way, rows], sent.at[sent_sem(0, p, way)],
            fr.at[full_sem(1, p, way, rslot(s, p, j))], nbr[a][way], device_id_type=MESH)

    def add_half(s, p, j, way):
        k = blk(shift(origin(s, p, j), ORDER[p][s], 1 if way == 0 else 3))
        rows = half_rows(p, way)
        G[0, k, rows] = (G[0, k, rows].astype(F32) + G[1, BASE[s] + j, rows].astype(F32)).astype(BF)
        rfull(s, p, j, way).start()

    def add_full(s, p, j):
        k = blk(origin(s, p, j))
        rows = part_rows(p)
        f = 21 + (BASE[s] + j) * 2
        G[0, k, rows] = (G[0, k, rows].astype(F32) + (
            G[1, f, rows].astype(F32) + G[1, f + 1, rows].astype(F32))).astype(BF)

    def start2(p, k):
        def one(i):
            rhalf(2, p, member(p, k, i), 0).start()
            rhalf(2, p, member(p, k, i), 1).start()
        loop(0, 4, one)

    def mid2(p, k):
        for w in range(2):
            settle(G.at[1, pl.ds(0, 4), half_rows(p, w)], fr.at[full_sem(0, p, w, slot(2, k))])
            loop(0, 4, lambda i, w=w: add_half(2, p, member(p, k, i), w))

    def end2(p, k):
        for w in range(2):
            settle(G.at[1, pl.ds(0, 4), part_rows(p)], fr.at[full_sem(1, p, w, slot(2, k))])
        loop(0, 4, lambda i: add_full(2, p, member(p, k, i)))

    def start(s, p, j):
        for w in range(2):
            rhalf(s, p, j, w).start()

    def mid(s, p, j):
        for w in range(2):
            rhalf(s, p, j, w).wait_recv()
            add_half(s, p, j, w)

    def end(s, p, j):
        for w in range(2):
            rfull(s, p, j, w).wait_recv()
        add_full(s, p, j)

    far = (2, 3, 1, 0)
    for i in range(1, 16):
        meta_copy(i).start()
    ev0 = gather_events(0)
    ev1 = gather_events(1)
    ev0[0]()
    fetch_weights()
    ev0[1]()
    ev0[2]()
    ev0[3]()
    settle(META.at[pl.ds(0, 15)], mr.at[0])
    settle(META.at[pl.ds(0, 15)], ms.at[0])
    for e in ev0[4:7]:
        e()
    prepare()
    for e in ev0[7:10]:
        e()
    ev1[0]()
    for e in ev0[10:]:
        e()
    for e in ev1[1:4]:
        e()
    gather_rest(0)
    loop(0, 4, lambda q: select(0, q))
    ev1[4]()
    ev1[5]()
    loop(4, 8, lambda q: select(0, q))
    ev1[6]()
    ev1[7]()
    settle_weights()
    loop(0, 2, gate_up)
    ev1[8]()
    ev1[9]()
    loop(2, 4, gate_up)
    ev1[10]()
    loop(0, 2, hidden)
    ev1[11]()
    loop(2, 4, hidden)
    gather_rest(1)
    loop(0, 8, lambda q: select(1, q))
    all_sent(0)
    all_sent(1)
    for a in range(3):
        for n in nbr[a]:
            pl.semaphore_signal(ready, inc=1, device_id=n, device_id_type=MESH)
    loop(0, 4, down)
    loop(0, 4, middle)
    loop(0, 4, lambda n: swap_d(n).wait_recv())

    def columns(b):
        y = (pos[1] + b) % 4
        loop(0, 4, lambda n: grad_x(n, y))
        loop(0, 8, lambda q: scatter(q, y))

    columns(2)
    pl.semaphore_wait(ready, 6)
    start2(0, 2)
    start2(1, 2)
    for k in far:
        start2(2, k)
    columns(3)
    start2(0, 3)
    start2(1, 3)
    mid2(0, 2)
    mid2(1, 2)
    columns(1)
    start2(0, 1)
    start2(1, 1)
    mid2(0, 3)
    mid2(1, 3)
    mid2(2, 2)
    mid2(2, 3)
    columns(0)
    start2(0, 0)
    start2(1, 0)
    mid2(2, 1)
    mid2(2, 0)
    mid2(0, 1)
    mid2(1, 1)
    gate_tokens()
    for i in range(1, 16):
        gate_one(i).start()
    end2(0, 2)
    loop(0, 4, lambda a: start(1, 0, a))
    end2(1, 2)
    start(1, 1, 2)
    end2(2, 2)
    loop(0, 4, lambda a: start(1, 2, a))
    mid2(0, 0)
    mid2(1, 0)
    settle(HID.at[:, pl.ds(0, 192)], th.at[0])
    loop(0, 4, grad_down)
    end2(1, 3)
    start(1, 1, 3)
    end2(1, 1)
    start(1, 1, 1)
    mid(1, 1, 2)
    for p in (0, 2):
        end2(p, 3)
        end2(p, 1)
        loop(0, 4, lambda a, p=p: mid(1, p, (a + 2) % 4))
    end2(1, 0)
    start(1, 1, 0)
    odd(lambda a: mid(1, 1, a))
    end2(0, 0)
    end2(2, 0)
    mid(1, 1, 0)
    for p in range(3):
        end(1, p, 2)
        start(0, p, 0)
    settle(GR.at[pl.ds(0, 15)], gr1.at[0])
    acc = GS[ex]
    for i in range(1, 16):
        acc = acc + GR[i]
    GT[...] = acc
    for i in range(1, 8):
        gate_two(i).start()
    for p in range(3):
        odd(lambda a, p=p: end(1, p, a))
        mid(0, p, 0)
    for p in range(3):
        end(1, p, 0)
    settle(GX.at[pl.ds(0, 7)], gr2.at[0])
    acc = GT[...]
    for i in range(1, 8):
        acc = acc + GX[i]
    gates[...] = acc / gpt[...]
    for p in range(3):
        end(0, p, 0)
    for c in range(4):
        dxo[:, c * 128:(c + 1) * 128] = G[0, me, c * 128:(c + 1) * 128, :]
    all_sent(0)
    settle(GR.at[pl.ds(0, 15)], gs1.at[0])
    settle(GX.at[pl.ds(0, 7)], gs2.at[0])
    settle(SND, es.at[0])
    settle(DT.at[:, :, pl.ds(0, 384)], ts.at[0])
    settle(HID.at[:, pl.ds(0, 192)], ts.at[1])
    for sem in (ol, osnd, orcv):
        settle(XS.at[:, pl.ds(0, 192)], sem.at[0])


def on_device(
    tokens, grad_out, expert_ids, gate_probs, seq_ids, log_ratio, advantages, w_gate, w_up, w_down
):
    vmem = pl.BlockSpec(memory_space=pltpu.VMEM)
    hbm = pl.BlockSpec(memory_space=pl.ANY)
    dma = lambda n: pltpu.SemaphoreType.DMA((n,))
    dx, gates, gd = pl.pallas_call(
        step_kernel,
        out_shape=(
            jax.ShapeDtypeStruct((128, 512), BF),
            jax.ShapeDtypeStruct((8, 128), F32),
            jax.ShapeDtypeStruct((4, 192, 4096), BF),
        ),
        in_specs=[pl.BlockSpec(memory_space=pltpu.SMEM)] + [vmem] * 6 + [hbm] * 3,
        out_specs=(vmem, vmem, hbm),
        scratch_shapes=[
            pltpu.VMEM((2, 64, 512, 128), BF),
            pltpu.VMEM((4, 384, 2048), BF),
            pltpu.VMEM((4, 384, 2048), BF),
            pltpu.VMEM((4, 1152, 2048), BF),
            pltpu.VMEM((4, 576, 384), F32),
            pltpu.VMEM((4, 576, 384), BF),
            pltpu.VMEM((4, 576, 384), BF),
            pltpu.VMEM((4, 384, 768), BF),
            pltpu.VMEM((4, 384, 384), BF),
            pltpu.VMEM((8, 192, 256), BF),
            pltpu.VMEM((8, 256, 192), BF),
            pltpu.VMEM((8, 192, 128), F32),
            pltpu.VMEM((16, 24, 128), F32),
            pltpu.VMEM((4, 8, 384), F32),
            pltpu.VMEM((16, 8, 128), F32),
            pltpu.VMEM((16, 8, 128), F32),
            pltpu.VMEM((8, 128), F32),
            pltpu.VMEM((8, 8, 128), F32),
            dma(2), dma(12), dma(108), dma(72), dma(1), dma(1), dma(1), dma(1), dma(1),
            dma(1), dma(8), dma(2), dma(4), dma(1), dma(1), dma(1), dma(1), dma(1), dma(1), dma(1), dma(1),
            pltpu.SemaphoreType.REGULAR,
        ],
        compiler_params=pltpu.CompilerParams(
            collective_id=0, has_side_effects=True, vmem_limit_bytes=67043328),
        name="expert_step",
    )(
        advantages, tokens, grad_out, expert_ids.T, gate_probs.T, seq_ids.reshape(1, -1), log_ratio.reshape(1, -1),
        w_gate, w_up, w_down)
    return dx, gates.T, gd


def solution(mesh):
    return jax.shard_map(
        on_device,
        mesh=mesh,
        in_specs=(
            P("expert", "dp"),
            P("expert", "dp"),
            P("expert", None),
            P("expert", None),
            P("expert"),
            P("expert"),
            P(),
            P("expert", "dp", None),
            P("expert", "dp", None),
            P("expert", "dp", None),
        ),
        out_specs=(P("expert", "dp"), P("expert", None), P("expert", "dp", None)),
        check_vma=False,
    )
```

time: 166 us -> 144 us (0.87)
  Pallas kernels: 151 us -> 134 us
  other arithmetic: 2.64 us -> 0 us
  local copies, waits for them, and re-layouts: 11 us -> 9.12 us
    pallas_call x1, Pallas kernels: 151 us -> 134 us  [on_device(): pl.pallas_call(step_kernel, out_shape=(jax.ShapeDtypeStruct((128, 512), B...]
    concatenate x1 -> x0, local copies, waits for them, and re-layouts: 3.13 us -> none  [on_device(): jnp.concatenate([expert_ids.astype(F32).T, gate_probs.T, seq_ids.astype(F...]
    unnamed x2 -> x3, local copies, waits for them, and re-layouts: 7.85 us -> 9.12 us
where the time goes in v2:
time: 144 us
  Pallas kernels  134 us (93%)
  local copies, waits for them, and re-layouts  9.12 us (6%)
    pallas_call x1, Pallas kernels, on_device(): pl.pallas_call(step_kernel, out_shape=(jax.ShapeDtypeStruct((128, 512), B...  134 us
    unnamed x3, local copies, waits for them, and re-layouts  9.12 us

profile of v2, /device:TPU:0, one launch (start us, length us, event | category | flops | bytes accessed | tf_op | source)
XLA Modules:
  0.0 143.6 jit_solution(7759498226302347938)
XLA Ops:
  0.6 133.8 %expert_step.1 = (bf16[128,512]{1,0:T(8,128)(2,1)}, f32[8,128]{1,0:T(8,128)}, bf16[4,192,4096]{2,1,0:T(8,128)(2,1)}) custom-call(f32[8]{0:T(128)} %adv.1, bf16[128,512]{1,0:T(8,128)(2,1)} %tok.1, bf16[128,512]{1,0:T(8,128)(2,1)} %gout.1, s32[8,128]{1,0:T(8,128)} %bitcast.6, f32[8,128]{1,0:T(8,128)} %bitcast.7, s32[1,128]{1,0:T(1,128)} %bitcast.8, ...), custom_call_target="tpu_custom_call" | custom-call | tf_op jit(solution)/shard_map/expert_step/pallas_call | solution.py:581
  134.5 1.6 %copy.16 = bf16[128,512]{1,0:T(8,128)(2,1)} copy(bf16[128,512]{1,0:T(8,128)(2,1)} %get-tuple-element.12) | data formatting | bytes 262144
  136.0 1.3 copy.17
  137.3 6.3 %copy.18 = bf16[4,192,4096]{2,1,0:T(8,128)(2,1)} copy(bf16[4,192,4096]{2,1,0:T(8,128)(2,1)} %get-tuple-element.14) | data formatting | bytes 12582912

commit v3 on v2

--- a/solution.py
+++ b/solution.py
@@ -14,7 +14,10 @@
 MESH = pl.DeviceIdType.MESH
 BF = jnp.bfloat16
 F32 = jnp.float32
-PARTS = ((0, 176, 96), (176, 176, 80), (352, 160, 80))
+PARTS = (
+    ((0, 176, 96), (176, 176, 80), (352, 160, 80)),
+    ((0, 176, 80), (176, 160, 80), (336, 176, 96)),
+)
 ORDER = ((0, 1, 2), (1, 2, 0), (2, 0, 1))
 BASE = (0, 1, 5)
 COUNT = (1, 4, 16)
@@ -102,7 +105,7 @@
         return (0, 1, 5)[s] + k
 
     def full_sem(v, p, way, k):
-        return ((v * 3 + p) * 2 + way) * 9 + k
+        return ((v * 3 + p) * 2 + way) * 10 + k
 
     def half_sem(v, p, way, k):
         return ((v * 3 + p) * 2 + way) * 6 + k
@@ -110,15 +113,18 @@
     def sent_sem(v, p, way):
         return (v * 3 + p) * 2 + way
 
-    def half_rows(p, way):
-        r0, n, h = PARTS[p]
+    def half_rows(p, way, v=0):
+        r0, n, h = PARTS[v][p]
         return pl.ds(r0, h) if way == 0 else pl.ds(r0 + h, n - h)
 
-    def part_rows(p):
-        return pl.ds(PARTS[p][0], PARTS[p][1])
+    def half_count(v, p, way):
+        return PARTS[v][p][2] if way == 0 else PARTS[v][p][1] - PARTS[v][p][2]
+
+    def part_rows(p, v=0):
+        return pl.ds(PARTS[v][p][0], PARTS[v][p][1])
 
     def full(v, s, p, j, way):
-        ref = G.at[v, blk(origin(s, p, j)), part_rows(p)]
+        ref = G.at[v, blk(origin(s, p, j)), part_rows(p, v)]
         k = slot(s, j // 4 if s == 2 else j)
         return pltpu.make_async_remote_copy(
             ref, ref, sent.at[sent_sem(v, p, way)], fr.at[full_sem(v, p, way, k)], nbr[ORDER[p][s]][way],
@@ -127,7 +133,7 @@
     def half(v, s, p, j, way):
         a = ORDER[p][s]
         b = blk(shift(origin(s, p, j), a, 3 if way == 0 else 1))
-        ref = G.at[v, b, half_rows(p, way)]
+        ref = G.at[v, b, half_rows(p, way, v)]
         k = 5 if s == 2 else slot(s, j)
         return pltpu.make_async_remote_copy(
             ref, ref, sent.at[sent_sem(v, p, way)], hr.at[half_sem(v, p, way, k)], nbr[a][way],
@@ -162,7 +168,7 @@
     def hop_bundle(v, b):
         for p in range(3):
             for w in range(2):
-                settle(G.at[v, pl.ds(0, 4), part_rows(p)], fr.at[full_sem(v, p, w, slot(2, b))])
+                settle(G.at[v, pl.ds(0, 4), part_rows(p, v)], fr.at[full_sem(v, p, w, slot(2, b))])
                 loop(0, 4, lambda a, p=p, w=w: half(v, 2, p, group(a, b), w).start())
 
     def last(v, s, j):
@@ -186,14 +192,12 @@
 
     def gather_rest(v):
         def one(p, w):
-            h = PARTS[p][2] if w == 0 else PARTS[p][1] - PARTS[p][2]
-            settle(G.at[v, pl.ds(0, 16), pl.ds(0, h)], hr.at[half_sem(v, p, w, 5)])
+            settle(G.at[v, pl.ds(0, 16), pl.ds(0, half_count(v, p, w))], hr.at[half_sem(v, p, w, 5)])
         each(one)
 
     def all_sent(v):
         def one(p, w):
-            h = PARTS[p][2] if w == 0 else PARTS[p][1] - PARTS[p][2]
-            settle(G.at[v, pl.ds(0, 21), pl.ds(0, PARTS[p][1] + h)], sent.at[sent_sem(v, p, w)])
+            settle(G.at[v, pl.ds(0, 21), pl.ds(0, PARTS[v][p][1] + half_count(v, p, w))], sent.at[sent_sem(v, p, w)])
         each(one)
 
     def meta_copy(i):
@@ -367,32 +371,29 @@
     def member(p, k, i):
         return group(k, i) if p == 1 else group(i, k)
 
-    def rslot(s, p, j):
-        if s < 2:
-            return slot(s, j)
-        return slot(2, j % 4 if p == 1 else j // 4)
-
-    def rhalf(s, p, j, way):
+    def rhalf(s, p, j, way, k=0):
         a = ORDER[p][s]
-        k = blk(shift(origin(s, p, j), a, 2))
+        b = blk(shift(origin(s, p, j), a, 2))
         rows = half_rows(p, way)
-        return pltpu.make_async_remote_copy(
-            G.at[0, k, rows], G.at[1, BASE[s] + j, rows], sent.at[sent_sem(0, p, way)],
-            fr.at[full_sem(0, p, way, rslot(s, p, j))], nbr[a][way], device_id_type=MESH)
-
-    def rfull(s, p, j, way):
+        sem = slot(2, k) if s == 2 else slot(s, j)
+        return pltpu.make_async_remote_copy(
+            G.at[0, b, rows], G.at[1, BASE[s] + j, rows], sent.at[sent_sem(0, p, way)],
+            fr.at[full_sem(0, p, way, sem)], nbr[a][way], device_id_type=MESH)
+
+    def rfull(s, p, j, way, k=0):
         a = ORDER[p][s]
-        k = blk(shift(origin(s, p, j), a, 1 if way == 0 else 3))
+        b = blk(shift(origin(s, p, j), a, 1 if way == 0 else 3))
         rows = part_rows(p)
-        return pltpu.make_async_remote_copy(
-            G.at[0, k, rows], G.at[1, 21 + (BASE[s] + j) * 2 + way, rows], sent.at[sent_sem(0, p, way)],
-            fr.at[full_sem(1, p, way, rslot(s, p, j))], nbr[a][way], device_id_type=MESH)
-
-    def add_half(s, p, j, way):
+        sem = slot(2, k) if s == 2 else slot(s, j)
+        return pltpu.make_async_remote_copy(
+            G.at[0, b, rows], G.at[1, 21 + (BASE[s] + j) * 2 + way, rows], sent.at[sent_sem(0, p, way)],
+            fr.at[full_sem(1, p, way, sem)], nbr[a][way], device_id_type=MESH)
+
+    def add_half(s, p, j, way, f=0):
         k = blk(shift(origin(s, p, j), ORDER[p][s], 1 if way == 0 else 3))
         rows = half_rows(p, way)
         G[0, k, rows] = (G[0, k, rows].astype(F32) + G[1, BASE[s] + j, rows].astype(F32)).astype(BF)
-        rfull(s, p, j, way).start()
+        rfull(s, p, j, way, f).start()
 
     def add_full(s, p, j):
         k = blk(origin(s, p, j))
@@ -403,19 +404,53 @@
 
     def start2(p, k):
         def one(i):
-            rhalf(2, p, member(p, k, i), 0).start()
-            rhalf(2, p, member(p, k, i), 1).start()
+            rhalf(2, p, member(p, k, i), 0, k).start()
+            rhalf(2, p, member(p, k, i), 1, k).start()
         loop(0, 4, one)
 
-    def mid2(p, k):
+    def halves_in(p, k):
         for w in range(2):
             settle(G.at[1, pl.ds(0, 4), half_rows(p, w)], fr.at[full_sem(0, p, w, slot(2, k))])
-            loop(0, 4, lambda i, w=w: add_half(2, p, member(p, k, i), w))
-
-    def end2(p, k):
+
+    def pass_on(p, k, i, f):
         for w in range(2):
-            settle(G.at[1, pl.ds(0, 4), part_rows(p)], fr.at[full_sem(1, p, w, slot(2, k))])
-        loop(0, 4, lambda i: add_full(2, p, member(p, k, i)))
+            add_half(2, p, member(p, k, i), w, f)
+
+    def mid2(p, step):
+        if step == 0:
+            halves_in(p, 2)
+            loop(0, 4, lambda i: pass_on(p, 2, (i + 2) % 4, 0))
+        elif step == 1:
+            halves_in(p, 3)
+            loop(1, 4, lambda i: pass_on(p, 3, i, 1))
+        elif step == 2:
+            halves_in(p, 1)
+            loop(1, 4, lambda i: pass_on(p, 1, i, 1))
+        elif step == 3:
+            halves_in(p, 0)
+            pass_on(p, 0, 2, 2)
+        elif step == 4:
+            odd(lambda k: pass_on(p, k, 0, 3))
+            odd(lambda i: pass_on(p, 0, i, 3))
+        else:
+            pass_on(p, 0, 0, 4)
+
+    def end2(p, f):
+        n = (4, 6, 1, 4, 1)[f]
+        for w in range(2):
+            settle(G.at[1, pl.ds(0, n), part_rows(p)], fr.at[full_sem(1, p, w, slot(2, f))])
+        take = lambda k, i: add_full(2, p, member(p, k, i))
+        if f == 0:
+            loop(0, 4, lambda i: take(2, i))
+        elif f == 1:
+            odd(lambda k: loop(1, 4, lambda i: take(k, i)))
+        elif f == 2:
+            take(0, 2)
+        elif f == 3:
+            odd(lambda k: take(k, 0))
+            odd(lambda i: take(0, i))
+        else:
+            take(0, 0)
 
     def start(s, p, j):
         for w in range(2):
@@ -494,53 +529,40 @@
     columns(3)
     start2(0, 3)
     start2(1, 3)
-    mid2(0, 2)
-    mid2(1, 2)
     columns(1)
     start2(0, 1)
     start2(1, 1)
-    mid2(0, 3)
-    mid2(1, 3)
-    mid2(2, 2)
-    mid2(2, 3)
+    for p in range(3):
+        mid2(p, 0)
     columns(0)
     start2(0, 0)
     start2(1, 0)
-    mid2(2, 1)
-    mid2(2, 0)
-    mid2(0, 1)
-    mid2(1, 1)
+    for p in range(3):
+        end2(p, 0)
+        if p == 1:
+            start(1, 1, 2)
+        else:
+            loop(0, 4, lambda a, p=p: start(1, p, (a + 2) % 4))
+    for p in range(3):
+        mid2(p, 1)
     gate_tokens()
     for i in range(1, 16):
         gate_one(i).start()
-    end2(0, 2)
-    loop(0, 4, lambda a: start(1, 0, a))
-    end2(1, 2)
-    start(1, 1, 2)
-    end2(2, 2)
-    loop(0, 4, lambda a: start(1, 2, a))
-    mid2(0, 0)
-    mid2(1, 0)
+    for p in range(3):
+        mid2(p, 2)
+    mid(1, 1, 2)
+    for p in range(3):
+        mid2(p, 3)
     settle(HID.at[:, pl.ds(0, 192)], th.at[0])
     loop(0, 4, grad_down)
-    end2(1, 3)
-    start(1, 1, 3)
-    end2(1, 1)
-    start(1, 1, 1)
-    mid(1, 1, 2)
-    for p in (0, 2):
-        end2(p, 3)
+    for p in range(3):
         end2(p, 1)
-        loop(0, 4, lambda a, p=p: mid(1, p, (a + 2) % 4))
-    end2(1, 0)
-    start(1, 1, 0)
-    odd(lambda a: mid(1, 1, a))
-    end2(0, 0)
-    end2(2, 0)
-    mid(1, 1, 0)
-    for p in range(3):
-        end(1, p, 2)
-        start(0, p, 0)
+        if p == 1:
+            odd(lambda a: start(1, 1, a))
+        else:
+            loop(1, 4, lambda a, p=p: mid(1, p, a))
+    for p in range(3):
+        mid2(p, 4)
     settle(GR.at[pl.ds(0, 15)], gr1.at[0])
     acc = GS[ex]
     for i in range(1, 16):
@@ -549,9 +571,21 @@
     for i in range(1, 8):
         gate_two(i).start()
     for p in range(3):
+        end2(p, 2)
+        if p == 1:
+            start(1, 1, 0)
+        end(1, p, 2)
+        start(0, p, 0)
+    for p in range(3):
+        mid2(p, 5)
+    odd(lambda a: mid(1, 1, a))
+    for p in range(3):
+        end2(p, 3)
+        mid(1, p, 0)
         odd(lambda a, p=p: end(1, p, a))
         mid(0, p, 0)
     for p in range(3):
+        end2(p, 4)
         end(1, p, 0)
     settle(GX.at[pl.ds(0, 7)], gr2.at[0])
     acc = GT[...]
@@ -570,6 +604,18 @@
     settle(HID.at[:, pl.ds(0, 192)], ts.at[1])
     for sem in (ol, osnd, orcv):
         settle(XS.at[:, pl.ds(0, 192)], sem.at[0])
+
+
+def store_kernel(gd, dx, gt, gdo, dxo, gto, B, DB, GB, arrive, leave):
+    pairs = [(gd.at[i // 4, pl.ds(i % 4 * 48, 48)], B.at[i], gdo.at[i // 4, pl.ds(i % 4 * 48, 48)]) for i in range(16)]
+    pairs += [(dx, DB, dxo), (gt, GB, gto)]
+    for i, (src, buf, dst) in enumerate(pairs):
+        pltpu.make_async_copy(src, buf, arrive.at[i]).start()
+    for i, (src, buf, dst) in enumerate(pairs):
+        pltpu.make_async_copy(src, buf, arrive.at[i]).wait()
+        pltpu.make_async_copy(buf, dst, leave.at[i]).start()
+    for i, (src, buf, dst) in enumerate(pairs):
+        pltpu.make_async_copy(buf, dst, leave.at[i]).wait()
 
 
 def on_device(
@@ -606,7 +652,7 @@
             pltpu.VMEM((16, 8, 128), F32),
             pltpu.VMEM((8, 128), F32),
             pltpu.VMEM((8, 8, 128), F32),
-            dma(2), dma(12), dma(108), dma(72), dma(1), dma(1), dma(1), dma(1), dma(1),
+            dma(2), dma(12), dma(120), dma(72), dma(1), dma(1), dma(1), dma(1), dma(1),
             dma(1), dma(8), dma(2), dma(4), dma(1), dma(1), dma(1), dma(1), dma(1), dma(1), dma(1), dma(1),
             pltpu.SemaphoreType.REGULAR,
         ],
@@ -616,6 +662,20 @@
     )(
         advantages, tokens, grad_out, expert_ids.T, gate_probs.T, seq_ids.reshape(1, -1), log_ratio.reshape(1, -1),
         w_gate, w_up, w_down)
+    gd, dx, gates = pl.pallas_call(
+        store_kernel,
+        out_shape=(
+            jax.ShapeDtypeStruct((4, 192, 4096), BF),
+            jax.ShapeDtypeStruct((128, 512), BF),
+            jax.ShapeDtypeStruct((8, 128), F32),
+        ),
+        in_specs=[hbm] * 3,
+        out_specs=(hbm,) * 3,
+        scratch_shapes=[
+            pltpu.VMEM((16, 48, 4096), BF), pltpu.VMEM((128, 512), BF), pltpu.VMEM((8, 128), F32), dma(18), dma(18),
+        ],
+        name="store_results",
+    )(gd, dx, gates)
     return dx, gates.T, gd
 
 

time: 144 us -> 141 us (0.979)
  local copies, waits for them, and re-layouts: 9.12 us -> 0 us
  Pallas kernels: 134 us -> 140 us
    unnamed x3 -> x0, local copies, waits for them, and re-layouts: 9.12 us -> none
    pallas_call x0 -> x1, Pallas kernels: none -> 5.55 us  [on_device(): pl.pallas_call(store_kernel, out_shape=(jax.ShapeDtypeStruct((4, 192, 409...]
where the time goes in v3:
time: 141 us
  Pallas kernels  140 us (99%)
    pallas_call x1, Pallas kernels, on_device(): pl.pallas_call(step_kernel, out_shape=(jax.ShapeDtypeStruct((128, 512), B...  135 us
    pallas_call x1, Pallas kernels, on_device(): pl.pallas_call(store_kernel, out_shape=(jax.ShapeDtypeStruct((4, 192, 409...  5.55 us

profile of v3, /device:TPU:0, one launch (start us, length us, event | category | flops | bytes accessed | tf_op | source)
XLA Modules:
  0.0 140.8 jit_solution(2248683029104731)
XLA Ops:
  0.6 134.6 %expert_step.1 = (bf16[128,512]{1,0:T(8,128)(2,1)}, f32[8,128]{1,0:T(8,128)}, bf16[4,192,4096]{2,1,0:T(8,128)(2,1)}) custom-call(f32[8]{0:T(128)} %adv.1, bf16[128,512]{1,0:T(8,128)(2,1)} %tok.1, bf16[128,512]{1,0:T(8,128)(2,1)} %gout.1, s32[8,128]{1,0:T(8,128)} %bitcast.5, f32[8,128]{1,0:T(8,128)} %bitcast.6, s32[1,128]{1,0:T(1,128)} %bitcast.7, ...), custom_call_target="tpu_custom_call" | custom-call | tf_op jit(solution)/shard_map/expert_step/pallas_call | solution.py:627
  135.3 5.5 %store_results.1 = (bf16[4,192,4096]{2,1,0:T(8,128)(2,1)}, bf16[128,512]{1,0:T(8,128)(2,1)}, f32[8,128]{1,0:T(8,128)}) custom-call(bf16[4,192,4096]{2,1,0:T(8,128)(2,1)} %get-tuple-element.9.gd, bf16[128,512]{1,0:T(8,128)(2,1)} %get-tuple-element.10.dx, f32[8,128]{1,0:T(8,128)} %get-tuple-element.11.gt), custom_call_target="tpu_custom_call" | custom-call | tf_op jit(solution)/shard_map/store_results/pallas_call | solution.py:665

commit v4 on v3

--- a/solution.py
+++ b/solution.py
@@ -189,6 +189,20 @@
         ev.append(lambda: odd(lambda b: hop_bundle(v, b)))
         ev.append(lambda: hop_bundle(v, 2))
         return ev
+
+    def early_events(v):
+        ev = []
+        ev.append(lambda: (send(v, 0, 0), send(v, 1, 0)))
+        ev.append(lambda: (hop(v, 0, 0), odd(lambda a: send(v, 1, a))))
+        ev.append(lambda: hop(v, 1, 0))
+        ev.append(lambda: (last(v, 0, 0), send(v, 1, 2)))
+        ev.append(lambda: odd(lambda a: hop(v, 1, a)))
+        ev.append(lambda: (last(v, 1, 0), hop(v, 1, 2)))
+        ev.append(lambda: (odd(lambda a: last(v, 1, a)), last(v, 1, 2)))
+        return ev
+
+    def late_sends(v, b):
+        loop(0, 4, lambda a: send(v, 2, group(a, b)))
 
     def gather_rest(v):
         def one(p, w):
@@ -470,7 +484,7 @@
     for i in range(1, 16):
         meta_copy(i).start()
     ev0 = gather_events(0)
-    ev1 = gather_events(1)
+    ev1 = early_events(1)
     ev0[0]()
     fetch_weights()
     ev0[1]()
@@ -478,31 +492,35 @@
     ev0[3]()
     settle(META.at[pl.ds(0, 15)], mr.at[0])
     settle(META.at[pl.ds(0, 15)], ms.at[0])
-    for e in ev0[4:7]:
-        e()
+    ev1[0]()
+    ev0[4]()
+    ev0[5]()
+    ev1[1]()
+    ev0[6]()
     prepare()
-    for e in ev0[7:10]:
-        e()
-    ev1[0]()
-    for e in ev0[10:]:
-        e()
-    for e in ev1[1:4]:
-        e()
+    ev1[2]()
+    ev0[7]()
+    ev1[3]()
+    ev0[8]()
+    ev1[4]()
+    ev0[9]()
+    ev1[5]()
+    ev0[10]()
+    ev1[6]()
+    ev0[11]()
+    for b in (0, 1, 3, 2):
+        late_sends(1, b)
     gather_rest(0)
     loop(0, 4, lambda q: select(0, q))
-    ev1[4]()
-    ev1[5]()
+    hop_bundle(1, 0)
     loop(4, 8, lambda q: select(0, q))
-    ev1[6]()
-    ev1[7]()
     settle_weights()
+    hop_bundle(1, 1)
     loop(0, 2, gate_up)
-    ev1[8]()
-    ev1[9]()
+    hop_bundle(1, 3)
     loop(2, 4, gate_up)
-    ev1[10]()
     loop(0, 2, hidden)
-    ev1[11]()
+    hop_bundle(1, 2)
     loop(2, 4, hidden)
     gather_rest(1)
     loop(0, 8, lambda q: select(1, q))
@@ -524,19 +542,21 @@
     pl.semaphore_wait(ready, 6)
     start2(0, 2)
     start2(1, 2)
-    for k in far:
-        start2(2, k)
+    start2(2, 2)
     columns(3)
     start2(0, 3)
     start2(1, 3)
+    start2(2, 3)
     columns(1)
     start2(0, 1)
     start2(1, 1)
+    start2(2, 1)
     for p in range(3):
         mid2(p, 0)
     columns(0)
     start2(0, 0)
     start2(1, 0)
+    start2(2, 0)
     for p in range(3):
         end2(p, 0)
         if p == 1:

time: 141 us -> 139 us (0.986)
    pallas_call x1, Pallas kernels: 135 us -> 133 us  [on_device(): pl.pallas_call(step_kernel, out_shape=(jax.ShapeDtypeStruct((128, 512), B...]
where the time goes in v4:
time: 139 us
  Pallas kernels  139 us (100%)
    pallas_call x1, Pallas kernels, on_device(): pl.pallas_call(step_kernel, out_shape=(jax.ShapeDtypeStruct((128, 512), B...  133 us
    pallas_call x1, Pallas kernels, on_device(): pl.pallas_call(store_kernel, out_shape=(jax.ShapeDtypeStruct((4, 192, 409...  5.55 us

profile of v4, /device:TPU:0, one launch (start us, length us, event | category | flops | bytes accessed | tf_op | source)
XLA Modules:
  0.0 139.2 jit_solution(4158637454211511211)
XLA Ops:
  0.6 133.0 %expert_step.1 = (bf16[128,512]{1,0:T(8,128)(2,1)}, f32[8,128]{1,0:T(8,128)}, bf16[4,192,4096]{2,1,0:T(8,128)(2,1)}) custom-call(f32[8]{0:T(128)} %adv.1, bf16[128,512]{1,0:T(8,128)(2,1)} %tok.1, bf16[128,512]{1,0:T(8,128)(2,1)} %gout.1, s32[8,128]{1,0:T(8,128)} %bitcast.5, f32[8,128]{1,0:T(8,128)} %bitcast.6, s32[1,128]{1,0:T(1,128)} %bitcast.7, ...), custom_call_target="tpu_custom_call" | custom-call | tf_op jit(solution)/shard_map/expert_step/pallas_call | solution.py:647
  133.7 5.5 %store_results.1 = (bf16[4,192,4096]{2,1,0:T(8,128)(2,1)}, bf16[128,512]{1,0:T(8,128)(2,1)}, f32[8,128]{1,0:T(8,128)}) custom-call(bf16[4,192,4096]{2,1,0:T(8,128)(2,1)} %get-tuple-element.9.gd, bf16[128,512]{1,0:T(8,128)(2,1)} %get-tuple-element.10.dx, f32[8,128]{1,0:T(8,128)} %get-tuple-element.11.gt), custom_call_target="tpu_custom_call" | custom-call | tf_op jit(solution)/shard_map/store_results/pallas_call | solution.py:685

commit v5 on v4

--- a/solution.py
+++ b/solution.py
@@ -565,14 +565,14 @@
             loop(0, 4, lambda a, p=p: start(1, p, (a + 2) % 4))
     for p in range(3):
         mid2(p, 1)
+    for p in range(3):
+        mid2(p, 2)
+    mid(1, 1, 2)
+    for p in range(3):
+        mid2(p, 3)
     gate_tokens()
     for i in range(1, 16):
         gate_one(i).start()
-    for p in range(3):
-        mid2(p, 2)
-    mid(1, 1, 2)
-    for p in range(3):
-        mid2(p, 3)
     settle(HID.at[:, pl.ds(0, 192)], th.at[0])
     loop(0, 4, grad_down)
     for p in range(3):

time: 139 us -> 139 us (level)
  no operation moved by 1% of the time
where the time goes in v5:
time: 139 us
  Pallas kernels  138 us (99%)
    pallas_call x1, Pallas kernels, on_device(): pl.pallas_call(step_kernel, out_shape=(jax.ShapeDtypeStruct((128, 512), B...  133 us
    pallas_call x1, Pallas kernels, on_device(): pl.pallas_call(store_kernel, out_shape=(jax.ShapeDtypeStruct((4, 192, 409...  5.55 us

profile of v5, /device:TPU:0, one launch (start us, length us, event | category | flops | bytes accessed | tf_op | source)
XLA Modules:
  0.0 138.8 jit_solution(15606970903039202485)
XLA Ops:
  0.6 132.6 %expert_step.1 = (bf16[128,512]{1,0:T(8,128)(2,1)}, f32[8,128]{1,0:T(8,128)}, bf16[4,192,4096]{2,1,0:T(8,128)(2,1)}) custom-call(f32[8]{0:T(128)} %adv.1, bf16[128,512]{1,0:T(8,128)(2,1)} %tok.1, bf16[128,512]{1,0:T(8,128)(2,1)} %gout.1, s32[8,128]{1,0:T(8,128)} %bitcast.5, f32[8,128]{1,0:T(8,128)} %bitcast.6, s32[1,128]{1,0:T(1,128)} %bitcast.7, ...), custom_call_target="tpu_custom_call" | custom-call | tf_op jit(solution)/shard_map/expert_step/pallas_call | solution.py:647
  133.2 5.5 %store_results.1 = (bf16[4,192,4096]{2,1,0:T(8,128)(2,1)}, bf16[128,512]{1,0:T(8,128)(2,1)}, f32[8,128]{1,0:T(8,128)}) custom-call(bf16[4,192,4096]{2,1,0:T(8,128)(2,1)} %get-tuple-element.9.gd, bf16[128,512]{1,0:T(8,128)(2,1)} %get-tuple-element.10.dx, f32[8,128]{1,0:T(8,128)} %get-tuple-element.11.gt), custom_call_target="tpu_custom_call" | custom-call | tf_op jit(solution)/shard_map/store_results/pallas_call | solution.py:685
